TPU v7x, 32 devices: a whole 2x2x4 slice. The times are simulated.
32 devices in a mesh: groups: 2 (over y), shot: 4 (over x, core), slab: 4 (over z).
Axes of the slice: x: 2, y: 2, z: 4, core: 2. Of those that a mesh axis runs over, the one named last changes fastest.
Arguments:
- slowness: float32 [32, 192, 128], P(('groups', 'slab')), parts along dimension 0, may hold values from 0.8 to 1.25
- wave_prev: float32 [8, 16, 192, 128], P(('groups', 'shot'), 'slab'), parts along dimension 0, may hold values from -6 to 6
- wave_now: float32 [8, 16, 192, 128], P(('groups', 'shot'), 'slab'), parts along dimension 0, may hold values from -6 to 6
- memory: float32 [8, 3, 16, 192, 128], P(('groups', 'shot'), None, 'slab'), parts along dimension 0, may hold values from -6 to 6
- adjoint_now: float32 [8, 16, 192, 128], P(('groups', 'shot'), 'slab'), parts along dimension 0, may hold values from -6 to 6
- adjoint_prev: float32 [8, 16, 192, 128], P(('groups', 'shot'), 'slab'), parts along dimension 0, may hold values from -6 to 6
- wavelet: float32 [4], replicated, may hold values from -16 to 16
- src_cells: int32 [8, 64], P(('groups', 'shot')), parts along dimension 0, may hold values from 0 to 393215
- src_signs: int32 [8, 64], P(('groups', 'shot')), parts along dimension 0, may hold values from -1 to 1, as said below
- rec_cells: int32 [512], P('groups'), parts along dimension 0, may hold values from 0 to 393215
- observed: float32 [8, 4, 256], P(('groups', 'shot')), parts along dimension 0, may hold values from -6 to 6
Outputs:
- new_slowness: float32 [32, 192, 128], P(('groups', 'slab')), parts along dimension 0
- gradient: float32 [32, 192, 128], P(('groups', 'slab'), 'shot'), parts along dimension 0
There are 2 independent parts, one for each index of `groups`. A program takes and returns all parts, laid end to end along the dimension named above; an argument that names none is the same for every part. Nothing has to cross between parts.
Inputs may be any that keep to these rules, and one draw needn't show every extreme that they name: `src_signs`: each entry is -1 or +1.
All inputs are finite; a program needn't handle non-finite values.
Results may differ from a plain program's by a relative error of at most 0.0001.
Values sent between devices are 32-bit elements; how exact they have to be, the bound alone decides.
No kernel may reach another device: no remote copies, remote signals or barrier semaphores. Data moves between devices by JAX's collectives and lax.ppermute only.
A program may use at most 64 MiB of HBM per device.

v0:
```python
import jax
import jax.numpy as jnp
from jax import lax
from jax.sharding import PartitionSpec as P

STEPS = 4


center_coef = -2.5
near_coef = 4.0 / 3.0
far_coef = -1.0 / 12.0
courant = 0.14
relax_decay = (0.3, 0.7, 0.95)
relax_weight = (0.3, 0.2, 0.1)
update_rate = 0.05
tiny_eps = 1e-06


def padded_2(block, sides, width):
    for axis, dim in sides:
        count = lax.axis_size(axis)
        forward = [(i, i + 1) for i in range(count - 1)]
        backward = [(target, source) for source, target in forward]
        low = lax.ppermute(
            lax.slice_in_dim(block, block.shape[dim] - width, None, axis=dim), axis, forward
        )
        high = lax.ppermute(lax.slice_in_dim(block, 0, width, axis=dim), axis, backward)
        block = jnp.concatenate([low, block, high], axis=dim)
    return block


def laplace(padded):
    middle = padded[2:-2]
    flanks = jnp.pad(middle, ((0, 0), (2, 2), (2, 2)))
    depth_sum = near_coef * (padded[3:-1] + padded[1:-3]) + far_coef * (padded[4:] + padded[:-4])
    cross_sum = near_coef * (flanks[:, 3:-1, 2:-2] + flanks[:, 1:-3, 2:-2]) + far_coef * (
        flanks[:, 4:, 2:-2] + flanks[:, :-4, 2:-2]
    )
    along_sum = near_coef * (flanks[:, 2:-2, 3:-1] + flanks[:, 2:-2, 1:-3]) + far_coef * (
        flanks[:, 2:-2, 4:] + flanks[:, 2:-2, :-4]
    )
    return 3.0 * center_coef * middle + depth_sum + cross_sum + along_sum


def place_sources(cells, signs, start, count):
    local = cells - start
    inside = (local >= 0) & (local < count)
    slot = jnp.where(inside, local, count)
    return jnp.zeros((count,), jnp.float32).at[slot].add(signs.astype(jnp.float32), mode="drop")


def per_device(
    slowness,
    wave_prev,
    wave_now,
    memory,
    adjoint_now,
    adjoint_prev,
    wavelet,
    src_cells,
    src_signs,
    rec_cells,
    observed,
):
    depth, width, lanes = slowness.shape
    plane = width * lanes
    block = depth * plane
    offset = lax.axis_index("slab") * block
    decay = jnp.array(relax_decay, jnp.float32)[:, None, None, None]
    weight = jnp.array(relax_weight, jnp.float32)[:, None, None, None]
    rec_local = rec_cells - offset
    rec_inside = (rec_local >= 0) & (rec_local < block)
    rec_slot = jnp.where(rec_inside, rec_local, block)
    rec_safe = jnp.minimum(rec_slot, block - 1)
    scaled = courant / (slowness * slowness)
    older, current, relax = (wave_prev[0], wave_now[0], memory[0])
    saved = []
    misfits = []

    def record(field, level):
        picked = field.reshape(-1)[rec_safe]
        misfits.append(jnp.where(rec_inside, picked - observed[0, level], 0.0))

    src_field = place_sources(src_cells[0], src_signs[0], offset, block).reshape(
        depth, width, lanes
    )
    for level in range(STEPS):
        padded = padded_2(current, (("slab", 0),), 2)
        curved = laplace(padded)
        accel = curved + jnp.sum(relax, 0)
        newer = 2.0 * current - older + scaled * accel + wavelet[level] * src_field
        relax = decay * relax - weight * curved[None]
        older, current = (current, newer)
        saved.append(accel)
        record(current, level)
    back_prev, back_now = (adjoint_prev[0], adjoint_now[0])
    back_relax = jnp.zeros_like(relax)
    accum = jnp.zeros_like(slowness)
    for level in reversed(range(STEPS)):
        inject = (
            jnp.zeros((block,), jnp.float32)
            .at[rec_slot]
            .add(misfits[level], mode="drop")
            .reshape(depth, width, lanes)
        )
        united = back_now + inject
        pushed = scaled * united
        drive = pushed - jnp.sum(weight * back_relax, 0)
        padded = padded_2(drive, (("slab", 0),), 2)
        accum = accum + united * saved[level]
        back_prev, back_now = (-united, back_prev + 2.0 * united + laplace(padded))
        back_relax = decay * back_relax + pushed[None]
    local_grad = accum * (-2.0 * courant / (slowness * slowness * slowness))
    cells_all = lax.axis_size("slab") * block
    share = width // lax.axis_size("shot")
    first = lax.axis_index("shot") * share
    summed = lax.psum(local_grad, "shot")
    squares = lax.psum(jnp.sum(summed * summed), "slab")
    rms_value = jnp.sqrt(squares / cells_all + tiny_eps)
    normed = summed / rms_value
    new_slowness = slowness - update_rate * normed
    gradient = lax.dynamic_slice_in_dim(normed, first, share, 1)
    return (new_slowness, gradient)


def solution(mesh):
    in_specs = (
        P(("groups", "slab"), None, None),
        P(("groups", "shot"), "slab", None, None),
        P(("groups", "shot"), "slab", None, None),
        P(("groups", "shot"), None, "slab", None, None),
        P(("groups", "shot"), "slab", None, None),
        P(("groups", "shot"), "slab", None, None),
        P(),
        P(("groups", "shot"), None),
        P(("groups", "shot"), None),
        P("groups"),
        P(("groups", "shot"), None, None),
    )
    out_specs = (P(("groups", "slab"), None, None), P(("groups", "slab"), "shot", None))
    return jax.shard_map(
        per_device, mesh=mesh, in_specs=in_specs, out_specs=out_specs, check_vma=False
    )
```

profile of v0, /device:TPU:0, one launch (start us, length us, event | category | flops | bytes accessed | tf_op | source)
XLA Modules:
  0.0 167.0 jit_solution(11458838551574252018)
XLA Ops:
  7.2 1.1 slice_bitcast_fusion.1
  8.3 1.3 collective-permute-start
  9.6 5.6 %collective-permute-start.1 = (f32[2,192,128]{2,1,0:T(8,128)S(1)}, f32[2,192,128]{2,1,0:T(8,128)S(1)}, u32[]{:S(2)}, u32[]{:S(2)}) collective-permute-start(f32[2,192,128]{2,1,0:T(8,128)S(1)} %get-tuple-element.43), channel_id=1, source_target_pairs={{0,1},{1,2},{2,3},{4,5},{5,6},{6,7},{8,9},{9,10},{10,11},{12,13},{... | collective-permute-start | bytes 589832 | tf_op jit(solution)/shard_map/ppermute | solution.py:24
  15.2 0.7 convert_bitcast_fusion
  15.8 1.5 fusion.182
  17.3 0.7 fusion.166
  17.9 1.4 reduce_sum.74
  19.4 1.0 scatter_custom_fusion
  20.4 2.6 %broadcast_multiply_fusion.1 = (f32[98304]{0:T(1024)S(1)}, f32[98304]{0:T(1024)S(1)}, f32[98304]{0:T(1024)S(1)}, f32[98304]{0:T(1024)S(1)}) fusion(f32[98304]{0:T(1024)S(1)} %scatter_custom_fusion, f32[]{:T(128)} %bitcast.13, f32[]{:T(128)} %bitcast.15, f32[]{:T(128)} %bitcast.11, f32[]{:T(128)} %bitcast.5), kind=kLoop, calls=%fused_computation.281 | loop fusion | flops 393216 | bytes 1966096 | tf_op jit(solution)/shard_map/mul | solution.py:91
  23.2 1.3 fusion.155
  24.5 1.3 collective-permute-start.2
  25.8 4.6 %collective-permute-start.3 = (f32[2,192,128]{2,1,0:T(8,128)S(1)}, f32[2,192,128]{2,1,0:T(8,128)S(1)}, u32[]{:S(2)}, u32[]{:S(2)}) collective-permute-start(f32[2,192,128]{2,1,0:T(8,128)S(1)} %get-tuple-element.41), channel_id=1, source_target_pairs={{0,1},{1,2},{2,3},{4,5},{5,6},{6,7},{8,9},{9,10},{10,11},{12,13},{... | collective-permute-start | bytes 589832 | tf_op jit(solution)/shard_map/ppermute | solution.py:24
  30.4 0.2 fusion.2
  30.6 2.1 %collective-permute-done.2 = f32[2,192,128]{2,1,0:T(8,128)S(1)} collective-permute-done((f32[2,192,128]{2,1,0:T(8,128)S(1)}, f32[2,192,128]{2,1,0:T(8,128)S(1)}, u32[]{:S(2)}, u32[]{:S(2)}) %collective-permute-start.2) | collective-permute-done | bytes 196640 | tf_op jit(solution)/shard_map/ppermute | solution.py:27
  32.7 1.2 collective-permute-done.3
  33.9 0.5 add_add_fusion.2
  34.5 1.3 collective-permute-start.4
  35.8 5.0 %collective-permute-start.5 = (f32[2,192,128]{2,1,0:T(8,128)S(1)}, f32[2,192,128]{2,1,0:T(8,128)S(1)}, u32[]{:S(2)}, u32[]{:S(2)}) collective-permute-start(f32[2,192,128]{2,1,0:T(8,128)S(1)} %get-tuple-element.35), channel_id=1, source_target_pairs={{0,1},{1,2},{2,3},{4,5},{5,6},{6,7},{8,9},{9,10},{10,11},{12,13},{... | collective-permute-start | bytes 589832 | tf_op jit(solution)/shard_map/ppermute | solution.py:24
  40.8 0.6 fusion.181
  41.4 1.1 collective-permute-done.4
  42.5 1.5 collective-permute-done.5
  44.0 0.5 fusion.52
  44.5 0.5 fusion.1
  45.0 0.2 add_add_fusion.1
  45.2 0.8 fusion.178
  45.9 1.3 collective-permute-start.6
  47.2 5.0 %collective-permute-start.7 = (f32[2,192,128]{2,1,0:T(8,128)}, f32[2,192,128]{2,1,0:T(8,128)S(1)}, u32[]{:S(2)}, u32[]{:S(2)}) collective-permute-start(f32[2,192,128]{2,1,0:T(8,128)} %get-tuple-element.33), channel_id=1, source_target_pairs={{0,1},{1,2},{2,3},{4,5},{5,6},{6,7},{8,9},{9,10},{10,11},{12,13},{... | collective-permute-start | bytes 589832 | tf_op jit(solution)/shard_map/ppermute | solution.py:24
  52.3 0.6 compare_select_fusion.1
  52.8 2.3 %gather_fusion.3 = f32[256]{0:T(256)} fusion(f32[98304]{0:T(1024)S(1)} %bitcast.58, s32[1024]{0:T(1024)S(1)} %pad_clamp_fusion), kind=kCustom, calls=%fused_computation.3 | custom fusion | bytes 3072 | tf_op jit(solution)/shard_map/gather | solution.py:81
  55.2 2.3 %gather_fusion.2 = f32[256]{0:T(256)} fusion(f32[98304]{0:T(1024)S(1)} %bitcast.57, s32[1024]{0:T(1024)S(1)} %pad_clamp_fusion), kind=kCustom, calls=%fused_computation.2 | custom fusion | bytes 3072 | tf_op jit(solution)/shard_map/gather | solution.py:81
  57.5 2.3 %gather_fusion.1 = f32[256]{0:T(256)} fusion(f32[98304]{0:T(1024)S(1)} %bitcast.59, s32[1024]{0:T(1024)S(1)} %pad_clamp_fusion), kind=kCustom, calls=%fused_computation.1 | custom fusion | bytes 3072 | tf_op jit(solution)/shard_map/gather | solution.py:81
  59.8 0.7 copy-done.6
  60.5 1.6 add_add_fusion
  62.2 1.7 %gather_fusion = f32[256]{0:T(256)S(1)} fusion(f32[98304]{0:T(1024)S(1)} %bitcast.61, s32[1024]{0:T(1024)S(1)} %pad_clamp_fusion), kind=kCustom, calls=%fused_computation | custom fusion | bytes 3072 | tf_op jit(solution)/shard_map/gather | solution.py:81
  63.9 1.3 subtract_select_fusion.1
  65.2 2.2 %scatter_custom_fusion.1 = f32[98304]{0:T(1024)S(1)} fusion(s32[256]{0:T(256)} %compare_select_fusion.1, f32[256]{0:T(256)S(1)} %get-tuple-element.51, f32[]{:T(128)} %constant.19.clone.1), kind=kCustom, calls=%fused_computation.292 | custom fusion | flops 256 | bytes 393728 | tf_op jit(solution)/shard_map/scatter-add | solution.py:103
  67.4 0.1 fusion.168
  67.5 0.8 fusion.177
  68.3 1.3 collective-permute-start.8
  69.6 4.6 %collective-permute-start.9 = (f32[2,192,128]{2,1,0:T(8,128)}, f32[2,192,128]{2,1,0:T(8,128)S(1)}, u32[]{:S(2)}, u32[]{:S(2)}) collective-permute-start(f32[2,192,128]{2,1,0:T(8,128)} %get-tuple-element.31), channel_id=1, source_target_pairs={{0,1},{1,2},{2,3},{4,5},{5,6},{6,7},{8,9},{9,10},{10,11},{12,13},{... | collective-permute-start | bytes 589832 | tf_op jit(solution)/shard_map/ppermute | solution.py:24
  74.1 2.2 %scatter_custom_fusion.2 = f32[98304]{0:T(1024)S(1)} fusion(s32[256]{0:T(256)} %compare_select_fusion.1, f32[256]{0:T(256)} %get-tuple-element.50, f32[]{:T(128)} %constant.19.clone.1), kind=kCustom, calls=%fused_computation.290 | custom fusion | flops 256 | bytes 393728 | tf_op jit(solution)/shard_map/scatter-add | solution.py:103
  76.3 1.3 collective-permute-done.9
  77.6 0.7 copy-done.11
  78.3 1.6 fusion.167
  79.9 1.1 multiply_reduce_fusion.1
  81.0 0.1 fusion.169
  81.1 1.3 collective-permute-start.10
  82.4 4.9 %collective-permute-start.11 = (f32[2,192,128]{2,1,0:T(8,128)S(1)}, f32[2,192,128]{2,1,0:T(8,128)S(1)}, u32[]{:S(2)}, u32[]{:S(2)}) collective-permute-start(f32[2,192,128]{2,1,0:T(8,128)S(1)} %get-tuple-element.29), channel_id=1, source_target_pairs={{0,1},{1,2},{2,3},{4,5},{5,6},{6,7},{8,9},{9,10},{10,11},{12,13},{... | collective-permute-start | bytes 589832 | tf_op jit(solution)/shard_map/ppermute | solution.py:24
  87.3 2.8 %scatter_custom_fusion.3 = f32[98304]{0:T(1024)} fusion(s32[256]{0:T(256)} %compare_select_fusion.1, f32[256]{0:T(256)} %get-tuple-element.48, f32[]{:T(128)} %constant.19.clone.1), kind=kCustom, calls=%fused_computation.288 | custom fusion | flops 256 | bytes 393728 | tf_op jit(solution)/shard_map/scatter-add | solution.py:103
  90.2 0.3 collective-permute-done.11
  90.5 0.4 copy-done.8
  90.9 0.3 copy-done.10
  91.2 1.8 %multiply_subtract_fusion.2 = (f32[4,192,128]{2,1,0:T(8,128)S(1)}, f32[4,192,128]{2,1,0:T(8,128)S(1)}) fusion(f32[4,192,128]{2,1,0:T(8,128)} %get-tuple-element.5, f32[4,192,128]{2,1,0:T(8,128)S(1)} %copy-done, f32[4,192,128]{2,1,0:T(8,128)} %bitcast.66, f32[4,192,128]{2,1,0:T(8,128)S(1)} %fusion.169, f32[2,192,128]{2,1,0:T(8,128)} %copy-done.10, ...), kind=kLoop, calls=%fused_computation.275 | loop fusion | flops 3145728 | bytes 3538944 | tf_op jit(solution)/shard_map/sub | solution.py:108
  93.0 0.8 fusion.175
  93.8 1.3 collective-permute-start.12
  95.1 5.7 %collective-permute-start.13 = (f32[2,192,128]{2,1,0:T(8,128)}, f32[2,192,128]{2,1,0:T(8,128)}, u32[]{:S(2)}, u32[]{:S(2)}) collective-permute-start(f32[2,192,128]{2,1,0:T(8,128)} %get-tuple-element.27), channel_id=1, source_target_pairs={{0,1},{1,2},{2,3},{4,5},{5,6},{6,7},{8,9},{9,10},{10,11},{12,13},{... | collective-permute-start | bytes 589832 | tf_op jit(solution)/shard_map/ppermute | solution.py:24
  100.8 2.2 %scatter_custom_fusion.4 = f32[98304]{0:T(1024)S(1)} fusion(s32[256]{0:T(256)} %compare_select_fusion.1, f32[256]{0:T(256)S(1)} %get-tuple-element.49, f32[]{:T(128)} %constant.19.clone.1), kind=kCustom, calls=%fused_computation.286 | custom fusion | flops 256 | bytes 393728 | tf_op jit(solution)/shard_map/scatter-add | solution.py:103
  103.0 0.6 collective-permute-done.13
  103.6 2.6 %fusion.4 = f32[4,192,128]{2,1,0:T(8,128)} fusion(f32[4,192,128]{2,1,0:T(8,128)S(1)} %copy-done, f32[4,192,128]{2,1,0:T(8,128)} %get-tuple-element.24, f32[4,192,128]{2,1,0:T(8,128)S(1)} %bitcast.65, f32[2,192,128]{2,1,0:T(8,128)} %collective-permute-done.13, f32[4,192,128]{2,1,0:T(8,128)S(1)} %get-tuple-element.8, ...), kind=kLoop, calls=%fused_computation.104 | loop fusion | flops 3833856 | bytes 4718592 | tf_op jit(solution)/shard_map/mul | solution.py:113
  106.2 36.8 %all-reduce.9.cloned.1.call-done = f32[4,192,128]{2,1,0:T(8,128)} async-done(((f32[4,192,128]{2,1,0:T(8,128)}), f32[4,192,128]{2,1,0:T(8,128)}) %all-reduce.9.cloned.1.call-update) | async-done | bytes 393232 | tf_op jit(solution)/shard_map/psum | solution.py:117
  143.0 1.7 %multiply_reduce_fusion.2 = f32[]{:T(128)} fusion(f32[4,192,128]{2,1,0:T(8,128)} %all-reduce.9.cloned.1.call-done), kind=kLoop, calls=%fused_computation.274 | loop fusion | flops 196607 | bytes 393220 | tf_op jit(solution)/shard_map/reduce_sum | solution.py:118
  144.7 12.3 %psum.15 = f32[]{:T(128)} all-reduce(f32[]{:T(128)} %multiply_reduce_fusion.2), channel_id=1, replica_groups=mesh['groups'=2,'shot'=4,'slab'=4] {'slab'}, use_global_device_ids=true, to_apply=%region_14.15 | all-reduce | flops 1 | bytes 8 | tf_op jit(solution)/shard_map/psum | solution.py:118
  157.7 1.8 %multiply_subtract_fusion.1 = (f32[4,192,128]{2,1,0:T(8,128)}, f32[4,192,128]{2,1,0:T(8,128)S(1)}) fusion(f32[4,192,128]{2,1,0:T(8,128)S(1)} %copy-done, f32[4,192,128]{2,1,0:T(8,128)} %all-reduce.9.cloned.1.call-done, f32[]{:T(128)S(6)} %sqrt.3), kind=kLoop, calls=%fused_computation.273 | loop fusion | flops 294912 | bytes 1572868 | tf_op jit(solution)/shard_map/sub | solution.py:121
  159.5 0.6 constant_dynamic-slice_fusion
  (44 shorter events, 0.3 us)
Async XLA Ops:
  7.2 135.9 %all-reduce.9.cloned.1.call-start = ((), (), s32[]{:S(2)}) async-start(), calls=%async_computation | async-start | bytes 786432 | tf_op jit(solution)/shard_map/psum | solution.py:117
  8.3 14.8 %collective-permute-start = (f32[2,192,128]{2,1,0:T(8,128)S(1)}, f32[2,192,128]{2,1,0:T(8,128)S(1)}, u32[]{:S(2)}, u32[]{:S(2)}) collective-permute-start(f32[2,192,128]{2,1,0:T(8,128)S(1)} %get-tuple-element.42), channel_id=1, source_target_pairs={{1,0},{2,1},{3,2},{5,4},{6,5},{7,6},{9,8},{10,9},{11,10},{13,12},{... | collective-permute-start | bytes 589832 | tf_op jit(solution)/shard_map/ppermute | solution.py:27
  9.6 13.5 %collective-permute-start.1 = (f32[2,192,128]{2,1,0:T(8,128)S(1)}, f32[2,192,128]{2,1,0:T(8,128)S(1)}, u32[]{:S(2)}, u32[]{:S(2)}) collective-permute-start(f32[2,192,128]{2,1,0:T(8,128)S(1)} %get-tuple-element.43), channel_id=1, source_target_pairs={{0,1},{1,2},{2,3},{4,5},{5,6},{6,7},{8,9},{9,10},{10,11},{12,13},{... | collective-permute-start | bytes 589832 | tf_op jit(solution)/shard_map/ppermute | solution.py:24
  19.3 3.7 %copy-start.14 = (s32[256]{0:T(256)S(1)}, s32[256]{0:T(256)}, u32[]{:S(2)}) copy-start(s32[256]{0:T(256)} %param.22) | copy-start | bytes 3076
  19.3 3.8 %copy-start = (f32[4,192,128]{2,1,0:T(8,128)S(1)}, f32[4,192,128]{2,1,0:T(8,128)}, u32[]{:S(2)}) copy-start(f32[4,192,128]{2,1,0:T(8,128)} %param.13) | copy-start | bytes 1179652
  19.4 3.8 %copy-start.2 = (f32[1,4,192,128]{3,2,1,0:T(8,128)S(1)}, f32[1,4,192,128]{3,2,1,0:T(8,128)}, u32[]{:S(2)}) copy-start(f32[1,4,192,128]{3,2,1,0:T(8,128)} %param.15) | copy-start | bytes 1179652
  19.4 3.8 %copy-start.5 = (f32[1,4,192,128]{3,2,1,0:T(8,128)S(1)}, f32[1,4,192,128]{3,2,1,0:T(8,128)}, u32[]{:S(2)}) copy-start(f32[1,4,192,128]{3,2,1,0:T(8,128)} %param.14) | copy-start | bytes 1179652
  23.1 7.2 %copy-start.1 = (f32[1,3,4,192,128]{4,3,2,1,0:T(8,128)S(1)}, f32[1,3,4,192,128]{4,3,2,1,0:T(8,128)}, u32[]{:S(2)}) copy-start(f32[1,3,4,192,128]{4,3,2,1,0:T(8,128)} %param.16) | copy-start | bytes 3538948
  23.1 7.2 %copy-start.12 = (f32[3]{0:T(128)S(1)}, f32[3]{0:T(128)}, u32[]{:S(2)}) copy-start(f32[3]{0:T(128)} %constant.18.clone) | copy-start | bytes 40
  23.2 7.2 %copy-start.13 = (f32[3]{0:T(128)S(1)}, f32[3]{0:T(128)}, u32[]{:S(2)}) copy-start(f32[3]{0:T(128)} %constant.50.clone) | copy-start | bytes 40
  24.5 8.3 %collective-permute-start.2 = (f32[2,192,128]{2,1,0:T(8,128)S(1)}, f32[2,192,128]{2,1,0:T(8,128)S(1)}, u32[]{:S(2)}, u32[]{:S(2)}) collective-permute-start(f32[2,192,128]{2,1,0:T(8,128)S(1)} %get-tuple-element.40), channel_id=1, source_target_pairs={{1,0},{2,1},{3,2},{5,4},{6,5},{7,6},{9,8},{10,9},{11,10},{13,12},{... | collective-permute-start | bytes 589832 | tf_op jit(solution)/shard_map/ppermute | solution.py:27
  25.8 8.1 %collective-permute-start.3 = (f32[2,192,128]{2,1,0:T(8,128)S(1)}, f32[2,192,128]{2,1,0:T(8,128)S(1)}, u32[]{:S(2)}, u32[]{:S(2)}) collective-permute-start(f32[2,192,128]{2,1,0:T(8,128)S(1)} %get-tuple-element.41), channel_id=1, source_target_pairs={{0,1},{1,2},{2,3},{4,5},{5,6},{6,7},{8,9},{9,10},{10,11},{12,13},{... | collective-permute-start | bytes 589832 | tf_op jit(solution)/shard_map/ppermute | solution.py:24
  33.9 6.9 %copy-start.16 = (f32[1,4,256]{2,1,0:T(4,128)S(1)}, f32[1,4,256]{2,1,0:T(4,128)}, u32[]{:S(2)}) copy-start(f32[1,4,256]{2,1,0:T(4,128)} %param.23) | copy-start | bytes 12292
  34.5 8.0 %collective-permute-start.4 = (f32[2,192,128]{2,1,0:T(8,128)S(1)}, f32[2,192,128]{2,1,0:T(8,128)S(1)}, u32[]{:S(2)}, u32[]{:S(2)}) collective-permute-start(f32[2,192,128]{2,1,0:T(8,128)S(1)} %get-tuple-element.34), channel_id=1, source_target_pairs={{1,0},{2,1},{3,2},{5,4},{6,5},{7,6},{9,8},{10,9},{11,10},{13,12},{... | collective-permute-start | bytes 589832 | tf_op jit(solution)/shard_map/ppermute | solution.py:27
  35.8 8.2 %collective-permute-start.5 = (f32[2,192,128]{2,1,0:T(8,128)S(1)}, f32[2,192,128]{2,1,0:T(8,128)S(1)}, u32[]{:S(2)}, u32[]{:S(2)}) collective-permute-start(f32[2,192,128]{2,1,0:T(8,128)S(1)} %get-tuple-element.35), channel_id=1, source_target_pairs={{0,1},{1,2},{2,3},{4,5},{5,6},{6,7},{8,9},{9,10},{10,11},{12,13},{... | collective-permute-start | bytes 589832 | tf_op jit(solution)/shard_map/ppermute | solution.py:24
  45.0 7.3 %copy-start.15 = (s32[256]{0:T(256)S(1)}, s32[256]{0:T(256)}, u32[]{:S(2)}) copy-start(s32[256]{0:T(256)} %param.22) | copy-start | bytes 3076
  45.9 13.8 %collective-permute-start.6 = (f32[2,192,128]{2,1,0:T(8,128)}, f32[2,192,128]{2,1,0:T(8,128)S(1)}, u32[]{:S(2)}, u32[]{:S(2)}) collective-permute-start(f32[2,192,128]{2,1,0:T(8,128)} %get-tuple-element.32), channel_id=1, source_target_pairs={{1,0},{2,1},{3,2},{5,4},{6,5},{7,6},{9,8},{10,9},{11,10},{13,12},{... | collective-permute-start | bytes 589832 | tf_op jit(solution)/shard_map/ppermute | solution.py:27
  47.2 12.5 %collective-permute-start.7 = (f32[2,192,128]{2,1,0:T(8,128)}, f32[2,192,128]{2,1,0:T(8,128)S(1)}, u32[]{:S(2)}, u32[]{:S(2)}) collective-permute-start(f32[2,192,128]{2,1,0:T(8,128)} %get-tuple-element.33), channel_id=1, source_target_pairs={{0,1},{1,2},{2,3},{4,5},{5,6},{6,7},{8,9},{9,10},{10,11},{12,13},{... | collective-permute-start | bytes 589832 | tf_op jit(solution)/shard_map/ppermute | solution.py:24
  59.8 0.7 copy-start.6
  59.8 0.7 copy-start.7
  62.2 5.2 %copy-start.4 = (f32[1,4,192,128]{3,2,1,0:T(8,128)S(1)}, f32[1,4,192,128]{3,2,1,0:T(8,128)}, u32[]{:S(2)}) copy-start(f32[1,4,192,128]{3,2,1,0:T(8,128)} %param.17) | copy-start | bytes 1179652
  67.4 10.9 %copy-start.3 = (f32[1,4,192,128]{3,2,1,0:T(8,128)S(1)}, f32[1,4,192,128]{3,2,1,0:T(8,128)}, u32[]{:S(2)}) copy-start(f32[1,4,192,128]{3,2,1,0:T(8,128)} %param.18) | copy-start | bytes 1179652
  68.3 8.1 %collective-permute-start.8 = (f32[2,192,128]{2,1,0:T(8,128)}, f32[2,192,128]{2,1,0:T(8,128)S(1)}, u32[]{:S(2)}, u32[]{:S(2)}) collective-permute-start(f32[2,192,128]{2,1,0:T(8,128)} %get-tuple-element.30), channel_id=1, source_target_pairs={{1,0},{2,1},{3,2},{5,4},{6,5},{7,6},{9,8},{10,9},{11,10},{13,12},{... | collective-permute-start | bytes 589832 | tf_op jit(solution)/shard_map/ppermute | solution.py:27
  69.6 8.0 %collective-permute-start.9 = (f32[2,192,128]{2,1,0:T(8,128)}, f32[2,192,128]{2,1,0:T(8,128)S(1)}, u32[]{:S(2)}, u32[]{:S(2)}) collective-permute-start(f32[2,192,128]{2,1,0:T(8,128)} %get-tuple-element.31), channel_id=1, source_target_pairs={{0,1},{1,2},{2,3},{4,5},{5,6},{6,7},{8,9},{9,10},{10,11},{12,13},{... | collective-permute-start | bytes 589832 | tf_op jit(solution)/shard_map/ppermute | solution.py:24
  76.3 1.3 copy-start.9
  77.6 0.7 copy-start.11
  81.1 9.1 %collective-permute-start.10 = (f32[2,192,128]{2,1,0:T(8,128)S(1)}, f32[2,192,128]{2,1,0:T(8,128)S(1)}, u32[]{:S(2)}, u32[]{:S(2)}) collective-permute-start(f32[2,192,128]{2,1,0:T(8,128)S(1)} %get-tuple-element.28), channel_id=1, source_target_pairs={{1,0},{2,1},{3,2},{5,4},{6,5},{7,6},{9,8},{10,9},{11,10},{13,12},{... | collective-permute-start | bytes 589832 | tf_op jit(solution)/shard_map/ppermute | solution.py:27
  82.4 8.1 %collective-permute-start.11 = (f32[2,192,128]{2,1,0:T(8,128)S(1)}, f32[2,192,128]{2,1,0:T(8,128)S(1)}, u32[]{:S(2)}, u32[]{:S(2)}) collective-permute-start(f32[2,192,128]{2,1,0:T(8,128)S(1)} %get-tuple-element.29), channel_id=1, source_target_pairs={{0,1},{1,2},{2,3},{4,5},{5,6},{6,7},{8,9},{9,10},{10,11},{12,13},{... | collective-permute-start | bytes 589832 | tf_op jit(solution)/shard_map/ppermute | solution.py:24
  90.2 0.7 copy-start.8
  90.5 0.7 copy-start.10
  93.8 9.2 %collective-permute-start.12 = (f32[2,192,128]{2,1,0:T(8,128)}, f32[2,192,128]{2,1,0:T(8,128)}, u32[]{:S(2)}, u32[]{:S(2)}) collective-permute-start(f32[2,192,128]{2,1,0:T(8,128)} %get-tuple-element.26), channel_id=1, source_target_pairs={{1,0},{2,1},{3,2},{5,4},{6,5},{7,6},{9,8},{10,9},{11,10},{13,12},{... | collective-permute-start | bytes 589832 | tf_op jit(solution)/shard_map/ppermute | solution.py:27
  95.1 8.5 %collective-permute-start.13 = (f32[2,192,128]{2,1,0:T(8,128)}, f32[2,192,128]{2,1,0:T(8,128)}, u32[]{:S(2)}, u32[]{:S(2)}) collective-permute-start(f32[2,192,128]{2,1,0:T(8,128)} %get-tuple-element.27), channel_id=1, source_target_pairs={{0,1},{1,2},{2,3},{4,5},{5,6},{6,7},{8,9},{9,10},{10,11},{12,13},{... | collective-permute-start | bytes 589832 | tf_op jit(solution)/shard_map/ppermute | solution.py:24
Sparse Core Ops, SparseCore 0:
  106.3 36.6 all-reduce.8
where the time goes:
time: 168 us; the launch traced here: 167 us
  waiting for transfers between devices  44.9 us (27%)
  starting transfers between devices  44.4 us (26%)
  other arithmetic  33.3 us (20%)
  local copies, waits for them, and re-layouts  17 us (10%)
  between operations  15.2 us (9%)
  blocking collectives  12.3 us (7%)
    psum x1, waiting for transfers between devices, per_device(): summed = lax.psum(local_grad, 'shot')  36.8 us
    ppermute x7, starting transfers between devices, padded_2(): lax.ppermute(lax.slice_in_dim(block, block.shape[dim] - width, None, axis...  35.4 us
    psum x1, blocking collectives, per_device(): squares = lax.psum(jnp.sum(summed * summed), 'slab')  12.3 us
    scatter-add x4, other arithmetic, per_device(): inject = jnp.zeros((block,), jnp.float32).at[rec_slot].add(misfits[level]...  9.37 us
    ppermute x7, starting transfers between devices, padded_2(): lax.ppermute(lax.slice_in_dim(block, 0, width, axis=dim), axis, backward)  9.01 us
    gather x4, local copies, waits for them, and re-layouts, record(): picked = field.reshape(-1)[rec_safe]  8.65 us
    ppermute x7, waiting for transfers between devices, padded_2(): lax.ppermute(lax.slice_in_dim(block, block.shape[dim] - width, None, axis...  4.85 us
    add x4, other arithmetic, per_device(): newer = 2.0 * current - older + scaled * accel + wavelet[level] * src_field  3.63 us
  transfers between devices with their start and end apart: 15, of which 8 were waited for; matrix products, arithmetic and copies ran while one was open for 14% of the time, Pallas kernels for 0%

commit v1 on v0

v1 whole, which is shorter than its diff:
```python
import jax
import jax.numpy as jnp
from jax import lax
from jax.experimental import pallas as pl
from jax.experimental.pallas import tpu as pltpu
from jax.sharding import PartitionSpec as P

STEPS = 4

center_coef = -2.5
near_coef = 4.0 / 3.0
far_coef = -1.0 / 12.0
courant = 0.14
relax_decay = (0.3, 0.7, 0.95)
relax_weight = (0.3, 0.2, 0.1)
update_rate = 0.05
tiny_eps = 1e-06

echo = tuple(
    sum(b * a**k for a, b in zip(relax_decay, relax_weight)) for k in range(STEPS)
)

PAD = 8
VMEM_SPEC = pl.BlockSpec(memory_space=pltpu.VMEM)
SMEM_SPEC = pl.BlockSpec(memory_space=pltpu.SMEM)
F32 = jnp.float32


def run(kernel, name, outs, args, scratch=(), smem=(), cost=200_000):
    specs = [SMEM_SPEC if i in smem else VMEM_SPEC for i in range(len(args))]
    return pl.pallas_call(
        kernel,
        name=name,
        out_shape=[jax.ShapeDtypeStruct(shape, F32) for shape in outs],
        in_specs=specs,
        out_specs=[VMEM_SPEC] * len(outs),
        scratch_shapes=list(scratch),
        compiler_params=pltpu.CompilerParams(vmem_limit_bytes=12 << 20),
        cost_estimate=pl.CostEstimate(flops=cost, bytes_accessed=cost, transcendentals=0),
    )(*args)


def chunks(width):
    step = 64 if width % 64 == 0 else 8
    return [(start, step) for start in range(0, width, step)]


def clear_pads(pad):
    depth, tall, lanes = pad.shape
    for p in range(depth):
        pad[p, :PAD] = jnp.zeros((PAD, lanes), F32)
        pad[p, tall - PAD :] = jnp.zeros((PAD, lanes), F32)


def own_laplace(pad, p, r, n):
    depth, _, lanes = pad.shape

    def at(plane, shift):
        return pad[plane, PAD + r + shift : PAD + r + shift + n]

    middle = at(p, 0)
    near = at(p, 1) + at(p, -1)
    far = at(p, 2) + at(p, -2)
    for plane in (p - 1, p + 1):
        if 0 <= plane < depth:
            near += at(plane, 0)
    for plane in (p - 2, p + 2):
        if 0 <= plane < depth:
            far += at(plane, 0)
    lane = lax.broadcasted_iota(jnp.int32, (n, lanes), 1)
    near += jnp.where(lane >= 1, pltpu.roll(middle, 1, 1), 0.0)
    near += jnp.where(lane < lanes - 1, pltpu.roll(middle, lanes - 1, 1), 0.0)
    far += jnp.where(lane >= 2, pltpu.roll(middle, 2, 1), 0.0)
    far += jnp.where(lane < lanes - 2, pltpu.roll(middle, lanes - 2, 1), 0.0)
    return 3.0 * center_coef * middle + near_coef * near + far_coef * far


def ghosts(a, b, r, n):
    slab, count = lax.axis_index("slab"), lax.axis_size("slab")
    even = lax.rem(slab, 2) == 0
    low, high = [], []
    for j in range(2):
        from_a, from_b = a[j, r : r + n], b[j, r : r + n]
        zero = jnp.zeros_like(from_a)
        low.append(jnp.where(slab == 0, zero, jnp.where(even, from_b, from_a)))
        high.append(jnp.where(slab == count - 1, zero, jnp.where(even, from_a, from_b)))
    return low, high


def reach(low, high, p, depth):
    terms = []
    for distance, coef in ((1, near_coef), (2, far_coef)):
        below, above = p - distance, p + distance
        if below < 0:
            terms.append(coef * low[2 + below])
        if above >= depth:
            terms.append(coef * high[above - depth])
    return sum(terms[1:], terms[0]) if terms else 0.0


def complete(low, high, scale_low, scale_high, field, r, n):
    depth = field.shape[0]

    def row(p):
        return field[p, r : r + n]

    low = [
        low[0] + scale_low[0, r : r + n] * (far_coef * row(0)),
        low[1] + scale_low[1, r : r + n] * (near_coef * row(0) + far_coef * row(1)),
    ]
    high = [
        high[0]
        + scale_high[0, r : r + n] * (near_coef * row(depth - 1) + far_coef * row(depth - 2)),
        high[1] + scale_high[1, r : r + n] * (far_coef * row(depth - 1)),
    ]
    return low, high


def send_planes(a, b, field):
    depth = field.shape[0]
    odd = lax.rem(lax.axis_index("slab"), 2)
    top = depth - 2
    for j in range(2):
        a[j] = field[top * (1 - odd) + j]
        b[j] = field[top * odd + j]


def one_hot_rows(cells, first_row, rows, lanes):
    shift = lanes.bit_length() - 1
    row = lax.shift_right_arithmetic(cells, shift) - first_row
    at = lax.broadcasted_iota(jnp.int32, (rows, cells.shape[1]), 0)
    return jnp.where(at == row, 1.0, 0.0).astype(jnp.bfloat16)


def is_lane(cells, lanes):
    at = lax.broadcasted_iota(jnp.int32, (lanes, cells.shape[1]), 0)
    return at == jnp.bitwise_and(cells, lanes - 1)


def spread(rows, columns):
    return lax.dot_general(
        rows, columns, (((1,), (1,)), ((), ())), preferred_element_type=F32
    )


def per_device(
    slowness,
    wave_prev,
    wave_now,
    memory,
    adjoint_now,
    adjoint_prev,
    wavelet,
    src_cells,
    src_signs,
    rec_cells,
    observed,
):
    depth, width, lanes = slowness.shape
    slabs, shots = lax.axis_size("slab"), lax.axis_size("shot")
    mechanisms = memory.shape[1]
    assert depth >= 4 and depth % 2 == 0 and lanes & (lanes - 1) == 0
    assert slabs & (slabs - 1) == 0 and shots & (shots - 1) == 0 and shots > 1 and slabs > 1
    whole, pair, half = (depth, width, lanes), (2, width, lanes), (depth // 2, width, lanes)
    rows = chunks(width)
    planes = range(depth)
    padded = pltpu.VMEM((depth, width + 2 * PAD, lanes), F32)
    older, now, relax = wave_prev[0], wave_now[0], memory[0]
    back_now, back_prev = adjoint_now[0], adjoint_prev[0]
    receivers = rec_cells.reshape(1, -1)
    seen = observed[0]

    pairs_a = [(i, i ^ 1) for i in range(slabs)]
    pairs_b = []
    for s in range(shots):
        for k in range(slabs):
            mate = k + 1 if k % 2 else k - 1
            if 0 <= mate < slabs:
                pairs_b.append((s * slabs + k, s * slabs + mate))
            else:
                pairs_b.append((s * slabs + k, (s ^ 1) * slabs + k))

    def exchange(sends):
        return lax.ppermute(sends[0], "slab", pairs_a), lax.ppermute(
            sends[1], ("shot", "slab"), pairs_b
        )

    def shot_swap(value, bit):
        return lax.ppermute(value, "shot", [(i, i ^ bit) for i in range(shots)])

    def slab_swap(value, bit):
        return lax.ppermute(value, "slab", [(i, i ^ bit) for i in range(slabs)])

    def first_sends(field, model, a, b):
        send_planes(a, b, field)
        odd = lax.rem(lax.axis_index("slab"), 2)
        mine = lax.rem(lax.axis_index("shot"), 2)
        top = depth - 2
        a[2] = model[top * (1 - odd) + mine]
        b[2] = model[top * odd + mine]

    got_now = exchange(run(first_sends, "sends0", [(3, width, lanes)] * 2, (now, slowness)))

    def step0(field, before, variables, model, cells, signs, pulse, *outs):
        lap, newer, scaled, factor, source, rest0, rest1, rest2, rest3, a, b, pad = outs
        rests = (rest0, rest1, rest2, rest3)
        clear_pads(pad)
        for p in planes:
            pad[p, PAD : PAD + width] = field[p]
        first_row = lax.axis_index("slab") * (depth * width)
        columns = jnp.where(is_lane(cells[...], lanes), signs[...].astype(F32), 0.0)
        columns = columns.astype(jnp.bfloat16)
        for p in planes:
            source[p] = spread(
                one_hot_rows(cells[...], first_row + p * width, width, lanes), columns
            )
        for p in planes:
            for r, n in rows:
                at = (p, slice(r, r + n))
                inverse = 1.0 / model[at]
                scale = courant * (inverse * inverse)
                scaled[at] = scale
                factor[at] = -2.0 * (scale * inverse)
                parts = [variables[(l, *at)] for l in range(mechanisms)]
                for n_step in range(STEPS):
                    terms = [
                        part if n_step == 0 else a_l**n_step * part
                        for part, a_l in zip(parts, relax_decay)
                    ]
                    rests[n_step][at] = sum(terms[1:], terms[0])
                curved = own_laplace(pad, p, r, n)
                lap[at] = curved
                newer[at] = (
                    2.0 * field[at]
                    - before[at]
                    + scale * (curved + rests[0][at])
                    + pulse[0] * source[at]
                )
        send_planes(a, b, newer)

    lap0s, p1s, scaled, factor, source, rest0, rest1, rest2, rest3, *sends = run(
        step0,
        "step0",
        [whole] * 9 + [pair] * 2,
        (now, older, relax, slowness, src_cells, src_signs, wavelet),
        [padded],
        smem=(6,),
    )
    got_p1 = exchange(sends)

    def receive(cells, values, *outs):
        first_row = lax.axis_index("slab") * (depth * width)
        lane = is_lane(cells[...], lanes)
        columns = [jnp.where(lane, 1.0, 0.0).astype(jnp.bfloat16)]
        for level in range(STEPS):
            left = values[level : level + 1, :]
            for _ in range(3):
                piece = left.astype(jnp.bfloat16)
                columns.append(jnp.where(lane, piece.astype(F32), 0.0).astype(jnp.bfloat16))
                left = left - piece.astype(F32)
        for p in planes:
            hot = one_hot_rows(cells[...], first_row + p * width, width, lanes)
            outs[0][p] = spread(hot, columns[0])
            for level in range(STEPS):
                first = 1 + 3 * level
                outs[1 + level][p] = (
                    spread(hot, columns[first + 2]) + spread(hot, columns[first + 1])
                ) + spread(hot, columns[first])

    counts, seen0, seen1, seen2, seen3 = run(
        receive, "receive", [whole] * 5, (receivers, seen), cost=2_000_000
    )

    def step1(a0, b0, field, lap_s, newer_s, scale, rest, rest_next, src, pulse, *outs):
        model_ghosts, lap, accel, newer, lap_next, newest, pad = outs
        clear_pads(pad)
        model_ghosts[0] = a0[2]
        model_ghosts[1] = b0[2]
        for r, n in rows:
            low, high = ghosts(a0, b0, r, n)
            for p in planes:
                at = (p, slice(r, r + n))
                outside = reach(low, high, p, depth)
                curved = lap_s[at] + outside
                lap[at] = curved
                accel[at] = curved + rest[at]
                value = newer_s[at] + scale[at] * outside
                newer[at] = value
                pad[p, PAD + r : PAD + r + n] = value
        for p in planes:
            for r, n in rows:
                at = (p, slice(r, r + n))
                curved = own_laplace(pad, p, r, n)
                lap_next[at] = curved
                newest[at] = (
                    2.0 * newer[at]
                    - field[at]
                    + scale[at] * (curved + (rest_next[at] - echo[0] * lap[at]))
                    + pulse[1] * src[at]
                )

    model_ghosts, lap0, accel0, p1, lap1s, p2s = run(
        step1,
        "step1",
        [pair] + [whole] * 5,
        (*got_now, now, lap0s, p1s, scaled, rest0, rest1, source, wavelet),
        [padded],
        smem=(9,),
    )
    partner_ghosts = shot_swap(model_ghosts, 1)

    def outer_scale(mine, other, low, high):
        slab, count = lax.axis_index("slab"), lax.axis_size("slab")
        even = lax.rem(slab, 2) == 0
        first = lax.rem(lax.axis_index("shot"), 2) == 0
        for r, n in rows:
            at = slice(r, r + n)
            for j in range(2):
                have = first if j == 0 else jnp.logical_not(first)
                from_a = jnp.where(have, mine[0, at], other[0, at])
                from_b = jnp.where(have, mine[1, at], other[1, at])
                for side, ref, at_end in (
                    (jnp.where(even, from_b, from_a), low, slab == 0),
                    (jnp.where(even, from_a, from_b), high, slab == count - 1),
                ):
                    value = courant / (side * side)
                    ref[j, at] = jnp.where(at_end, jnp.zeros_like(value), value)

    scale_low, scale_high = run(
        outer_scale, "outer_scale", [pair] * 2, (model_ghosts, partner_ghosts)
    )

    def step2(a1, b1, field, lap_s, newer_s, scale, s_low, s_high, rest, lap_old, *outs):
        lap, accel, newer, a, b = outs
        for r, n in rows:
            low, high = ghosts(a1, b1, r, n)
            low, high = complete(low, high, s_low, s_high, field, r, n)
            for p in planes:
                at = (p, slice(r, r + n))
                outside = reach(low, high, p, depth)
                curved = lap_s[at] + outside
                lap[at] = curved
                accel[at] = curved + (rest[at] - echo[0] * lap_old[at])
                newer[at] = newer_s[at] + scale[at] * outside
        send_planes(a, b, newer)

    lap1, accel1, p2, *sends = run(
        step2,
        "step2",
        [whole] * 3 + [pair] * 2,
        (*got_p1, now, lap1s, p2s, scaled, scale_low, scale_high, rest1, lap0),
    )
    got_p2 = exchange(sends)

    def step3(field, before, scale, rest, lap_a, lap_b, src, pulse, *outs):
        accel_s, newer, a, b, pad = outs
        clear_pads(pad)
        for p in planes:
            pad[p, PAD : PAD + width] = field[p]
        for p in planes:
            for r, n in rows:
                at = (p, slice(r, r + n))
                part = rest[at] - echo[0] * lap_b[at] - echo[1] * lap_a[at]
                accel = own_laplace(pad, p, r, n) + part
                accel_s[at] = accel
                newer[at] = (
                    2.0 * field[at] - before[at] + scale[at] * accel + pulse[2] * src[at]
                )
        send_planes(a, b, newer)

    accel2s, p3s, *sends = run(
        step3,
        "step3",
        [whole] * 2 + [pair] * 2,
        (p2, p1, scaled, rest2, lap0, lap1, source, wavelet),
        [padded],
        smem=(7,),
    )
    got_p3 = exchange(sends)

    def step4(a2, b2, field, accel_s, newer_s, scale, rest2_, rest3_, lap_a, lap_b, src, pulse, *outs):
        accel, newer, accel_next, newest, pad = outs
        clear_pads(pad)
        for r, n in rows:
            low, high = ghosts(a2, b2, r, n)
            for p in planes:
                at = (p, slice(r, r + n))
                outside = reach(low, high, p, depth)
                accel[at] = accel_s[at] + outside
                value = newer_s[at] + scale[at] * outside
                newer[at] = value
                pad[p, PAD + r : PAD + r + n] = value
        for p in planes:
            for r, n in rows:
                at = (p, slice(r, r + n))
                lap_c = accel[at] - (rest2_[at] - echo[0] * lap_b[at] - echo[1] * lap_a[at])
                part = rest3_[at] - echo[0] * lap_c - echo[1] * lap_b[at] - echo[2] * lap_a[at]
                acc = own_laplace(pad, p, r, n) + part
                accel_next[at] = acc
                newest[at] = (
                    2.0 * newer[at] - field[at] + scale[at] * acc + pulse[3] * src[at]
                )

    accel2, p3, accel3s, p4s = run(
        step4,
        "step4",
        [whole] * 4,
        (*got_p2, p2, accel2s, p3s, scaled, rest2, rest3, lap0, lap1, source, wavelet),
        [padded],
        smem=(11,),
    )

    def turn(a3, b3, field, accel_s, newer_s, scale, s_low, s_high, hits, sums, back, *outs):
        united, drive, total, a, b = outs
        for r, n in rows:
            low, high = ghosts(a3, b3, r, n)
            low, high = complete(low, high, s_low, s_high, field, r, n)
            for p in planes:
                at = (p, slice(r, r + n))
                outside = reach(low, high, p, depth)
                newest = newer_s[at] + scale[at] * outside
                value = back[at] + (hits[at] * newest - sums[at])
                united[at] = value
                drive[at] = scale[at] * value
                total[at] = value * (accel_s[at] + outside)
        send_planes(a, b, drive)

    united3, drive3, accum, *sends = run(
        turn,
        "turn",
        [whole] * 3 + [pair] * 2,
        (*got_p3, p2, accel3s, p4s, scaled, scale_low, scale_high, counts, seen3, back_now),
    )
    got_d3 = exchange(sends)

    def adjoint3(field, drive, back, scale, hits, pressure, sums, *outs):
        united, drive_next, a, b, pad = outs
        clear_pads(pad)
        for p in planes:
            pad[p, PAD : PAD + width] = drive[p]
        for p in planes:
            for r, n in rows:
                at = (p, slice(r, r + n))
                value = (
                    back[at]
                    + 2.0 * field[at]
                    + own_laplace(pad, p, r, n)
                    + (hits[at] * pressure[at] - sums[at])
                )
                united[at] = value
                drive_next[at] = scale[at] * value - echo[0] * drive[at]
        send_planes(a, b, drive_next)

    united2s, drive2s, *sends = run(
        adjoint3,
        "adjoint3",
        [whole] * 2 + [pair] * 2,
        (united3, drive3, back_prev, scaled, counts, p3, seen2),
        [padded],
    )
    got_d2 = exchange(sends)

    def adjoint2(
        a4, b4, united_s, drive_s, scale, drive_old, united_old, hits, pressure, sums, accel, acc, *outs
    ):
        united, drive, total, united_next, drive_next, pad = outs
        clear_pads(pad)
        for r, n in rows:
            low, high = ghosts(a4, b4, r, n)
            for p in planes:
                at = (p, slice(r, r + n))
                outside = reach(low, high, p, depth)
                value = united_s[at] + outside
                united[at] = value
                total[at] = acc[at] + value * accel[at]
                pushed = drive_s[at] + scale[at] * outside
                drive[at] = pushed
                pad[p, PAD + r : PAD + r + n] = pushed
        for p in planes:
            for r, n in rows:
                at = (p, slice(r, r + n))
                value = (
                    2.0 * united[at]
                    - united_old[at]
                    + own_laplace(pad, p, r, n)
                    + (hits[at] * pressure[at] - sums[at])
                )
                united_next[at] = value
                drive_next[at] = (
                    scale[at] * (value - echo[0] * united[at]) - echo[1] * drive_old[at]
                )

    united2, drive2, accum, united1s, drive1s = run(
        adjoint2,
        "adjoint2",
        [whole] * 5,
        (
            *got_d3,
            united2s,
            drive2s,
            scaled,
            drive3,
            united3,
            counts,
            p2,
            seen1,
            accel2,
            accum,
        ),
        [padded],
    )

    def adjoint1(a5, b5, drive_old, united_s, drive_s, scale, s_low, s_high, *outs):
        united, drive, a, b = outs
        for r, n in rows:
            low, high = ghosts(a5, b5, r, n)
            low, high = complete(low, high, s_low, s_high, drive_old, r, n)
            for p in planes:
                at = (p, slice(r, r + n))
                outside = reach(low, high, p, depth)
                united[at] = united_s[at] + outside
                drive[at] = drive_s[at] + scale[at] * outside
        send_planes(a, b, drive)

    united1, drive1, *sends = run(
        adjoint1,
        "adjoint1",
        [whole] * 2 + [pair] * 2,
        (*got_d2, drive3, united1s, drive1s, scaled, scale_low, scale_high),
    )
    got_d1 = exchange(sends)

    def adjoint0(drive, united, united_old, hits, pressure, sums, accel_b, accel_a, acc, *outs):
        total, pad = outs
        clear_pads(pad)
        for p in planes:
            pad[p, PAD : PAD + width] = drive[p]
        for p in planes:
            for r, n in rows:
                at = (p, slice(r, r + n))
                value = (
                    2.0 * united[at]
                    - united_old[at]
                    + own_laplace(pad, p, r, n)
                    + (hits[at] * pressure[at] - sums[at])
                )
                total[at] = acc[at] + united[at] * accel_b[at] + value * accel_a[at]

    (accum,) = run(
        adjoint0,
        "adjoint0",
        [whole],
        (drive1, united1, united2, counts, p1, seen0, accel1, accel0, accum),
        [padded],
    )

    def finish(a6, b6, acc, accel, fact, keep, send, grad):
        mine = lax.rem(lax.axis_index("shot"), 2)
        for r, n in rows:
            low, high = ghosts(a6, b6, r, n)
            for p in planes:
                at = (p, slice(r, r + n))
                outside = reach(low, high, p, depth)
                grad[at] = fact[at] * (acc[at] + accel[at] * outside)
        for j in range(depth // 2):
            keep[j] = grad[mine * (depth // 2) + j]
            send[j] = grad[(1 - mine) * (depth // 2) + j]

    keep, give = run(
        finish,
        "finish",
        [half] * 2,
        (*got_d1, accum, accel0, factor),
        [pltpu.VMEM(whole, F32)],
    )

    def add(x, y, out):
        out[...] = x[...] + y[...]

    (part,) = run(add, "add", [half], (keep, shot_swap(give, 1)))
    bit = 2
    while bit < shots:
        (part,) = run(add, "add", [half], (part, shot_swap(part, bit)))
        bit *= 2

    def gather(mine_ref, other_ref, total, squares):
        mine = lax.rem(lax.axis_index("shot"), 2)
        acc = jnp.zeros((8, lanes), F32)
        for j in range(depth // 2):
            for ref, place in ((mine_ref, mine), (other_ref, 1 - mine)):
                value = ref[j]
                total[place * (depth // 2) + j] = value
                acc += jnp.sum((value * value).reshape(width // 8, 8, lanes), axis=0)
        squares[...] = acc

    total, squares = run(
        gather, "gather", [whole, (8, lanes)], (part, shot_swap(part, 1))
    )

    def add4(w, x, y, z, out):
        out[...] = (w[...] + x[...]) + (y[...] + z[...])

    bit = 1
    others = []
    while bit < slabs:
        if others:
            (squares,) = run(add4 if len(others) == 3 else add, "add_squares", [(8, lanes)], (squares, *others))
        if 2 * bit < slabs:
            others = [slab_swap(squares, k * bit) for k in (1, 2, 3)]
            bit *= 4
        else:
            others = [slab_swap(squares, bit)]
            bit *= 2

    share = width // shots
    cells_all = slabs * depth * width * lanes

    def update(field, model, *refs):
        sums, (new_model, gradient) = refs[:-2], refs[-2:]
        acc = sums[0][...]
        for ref in sums[1:]:
            acc = acc + ref[...]
        power = jnp.sum(acc, axis=(0, 1), keepdims=True)
        inverse = 1.0 / jnp.sqrt(power / cells_all + tiny_eps)
        first = pl.multiple_of(lax.axis_index("shot") * share, 8)
        for p in planes:
            for r, n in rows:
                at = (p, slice(r, r + n))
                new_model[at] = model[at] - update_rate * (field[at] * inverse)
            gradient[p] = field[p, pl.ds(first, share)] * inverse

    return run(
        update,
        "update",
        [whole, (depth, share, lanes)],
        (total, slowness, squares, *others),
    )


def solution(mesh):
    in_specs = (
        P(("groups", "slab"), None, None),
        P(("groups", "shot"), "slab", None, None),
        P(("groups", "shot"), "slab", None, None),
        P(("groups", "shot"), None, "slab", None, None),
        P(("groups", "shot"), "slab", None, None),
        P(("groups", "shot"), "slab", None, None),
        P(),
        P(("groups", "shot"), None),
        P(("groups", "shot"), None),
        P("groups"),
        P(("groups", "shot"), None, None),
    )
    out_specs = (P(("groups", "slab"), None, None), P(("groups", "slab"), "shot", None))
    return jax.shard_map(
        lambda *args: tuple(per_device(*args)),
        mesh=mesh,
        in_specs=in_specs,
        out_specs=out_specs,
        check_vma=False,
    )
```

time: 168 us -> 71.2 us (0.42)
  other arithmetic: 33.3 us -> 0 us
  starting transfers between devices: 44.4 us -> 21.8 us
  waiting for transfers between devices: 44.9 us -> 29.8 us
  between operations: 15.2 us -> 0.76 us
  blocking collectives: 12.3 us -> 0 us
  Pallas kernels: 0 us -> 11.3 us
  local copies, waits for them, and re-layouts: 17 us -> 7.24 us
    psum x1 -> x0, waiting for transfers between devices: 36.8 us -> none  [per_device(): summed = lax.psum(local_grad, 'shot')]
    ppermute x14 -> x21, starting transfers between devices: 44.4 us -> 21.8 us  [the longest x7 15.3 us: exchange(): lax.ppermute(sends[0], 'slab', pairs_a)]
    ppermute x14 -> x21, waiting for transfers between devices: 8.05 us -> 29.8 us  [the longest x7 17.4 us: exchange(): lax.ppermute(sends[0], 'slab', pairs_a)]
    psum x1 -> x0, blocking collectives: 12.3 us -> none  [per_device(): squares = lax.psum(jnp.sum(summed * summed), 'slab')]
    pallas_call x0 -> x18, Pallas kernels: none -> 11.3 us  [run(): pl.pallas_call(kernel, name=name, out_shape=[jax.ShapeDtypeStruct(shape,...]
    scatter-add x5 -> x0, other arithmetic: 10.4 us -> none  [the longest x4 9.37 us: per_device(): inject = jnp.zeros((block,), jnp.float32).at[rec_slot].add(misfits[level]...]
    gather x4 -> x0, local copies, waits for them, and re-layouts: 8.65 us -> none  [record(): picked = field.reshape(-1)[rec_safe]]
    mul x4 -> x0, other arithmetic: 6.96 us -> none  [the longest x1 2.65 us: per_device(): newer = 2.0 * current - older + scaled * accel + wavelet[level] * src_field]
  transfers between devices with their start and end apart: 15 -> 21, of which waited for: 8 -> 12; matrix products, arithmetic and copies ran while one was open for 14% -> 0% of each run, Pallas kernels for 0% -> 11%
where the time goes in v1:
time: 71.2 us; the launch traced here: 70.9 us
  waiting for transfers between devices  29.8 us (42%)
  starting transfers between devices  21.8 us (31%)
  Pallas kernels  11.3 us (16%)
  local copies, waits for them, and re-layouts  7.24 us (10%)
  between operations  0.76 us (1%)
    ppermute x7, waiting for transfers between devices, exchange(): lax.ppermute(sends[0], 'slab', pairs_a)  17.4 us
    ppermute x7, starting transfers between devices, exchange(): lax.ppermute(sends[0], 'slab', pairs_a)  15.3 us
    pallas_call x18, Pallas kernels, run(): pl.pallas_call(kernel, name=name, out_shape=[jax.ShapeDtypeStruct(shape,...  11.3 us
    ppermute x4, waiting for transfers between devices, shot_swap(): return lax.ppermute(value, 'shot', [(i, i ^ bit) for i in range(shots)])  8.31 us
    unnamed x30, local copies, waits for them, and re-layouts  7.24 us
    ppermute x3, starting transfers between devices, slab_swap(): return lax.ppermute(value, 'slab', [(i, i ^ bit) for i in range(slabs)])  4.45 us
    ppermute x3, waiting for transfers between devices, slab_swap(): return lax.ppermute(value, 'slab', [(i, i ^ bit) for i in range(slabs)])  4.01 us
    ppermute x4, starting transfers between devices, shot_swap(): return lax.ppermute(value, 'shot', [(i, i ^ bit) for i in range(shots)])  1.86 us
  transfers between devices with their start and end apart: 21, of which 12 were waited for; matrix products, arithmetic and copies ran while one was open for 0% of the time, Pallas kernels for 11%

profile of v1, /device:TPU:0, one launch (start us, length us, event | category | flops | bytes accessed | tf_op | source)
XLA Modules:
  0.0 70.9 jit_solution(11584295338565300968)
XLA Ops:
  0.6 0.0 copy-start
  0.6 1.0 %copy-done = f32[1,4,192,128]{3,2,1,0:T(8,128)S(1)} copy-done((f32[1,4,192,128]{3,2,1,0:T(8,128)S(1)}, f32[1,4,192,128]{3,2,1,0:T(8,128)}, u32[]{:S(2)}) %copy-start) | copy-done | bytes 393240
  1.6 1.0 %copy-done.2 = f32[4,192,128]{2,1,0:T(8,128)S(1)} copy-done((f32[4,192,128]{2,1,0:T(8,128)S(1)}, f32[4,192,128]{2,1,0:T(8,128)}, u32[]{:S(2)}) %copy-start.2) | copy-done | bytes 393240
  2.7 3.1 %collective-permute-start.2 = (f32[3,192,128]{2,1,0:T(8,128)S(1)}, f32[3,192,128]{2,1,0:T(8,128)S(1)}, u32[]{:S(2)}, u32[]{:S(2)}) collective-permute-start(f32[3,192,128]{2,1,0:T(8,128)S(1)} %get-tuple-element.64), channel_id=1, source_target_pairs={{0,1},{1,0},{2,3},{3,2},{4,5},{5,4},{6,7},{7,6},{8,9},{9,8},{10,11... | collective-permute-start | bytes 884744 | tf_op jit(solution)/shard_map/ppermute | solution.py:184
  5.8 0.0 collective-permute-start.3
  5.8 1.0 %copy-done.3 = f32[4,192,128]{2,1,0:T(8,128)S(1)} copy-done((f32[4,192,128]{2,1,0:T(8,128)S(1)}, f32[4,192,128]{2,1,0:T(8,128)}, u32[]{:S(2)}) %copy-start.3) | copy-done | bytes 393240
  6.8 1.3 %copy-done.5 = f32[1,3,4,192,128]{4,3,2,1,0:T(8,128)S(1)} copy-done((f32[1,3,4,192,128]{4,3,2,1,0:T(8,128)S(1)}, f32[1,3,4,192,128]{4,3,2,1,0:T(8,128)}, u32[]{:S(2)}) %copy-start.5) | copy-done | bytes 1179672
  8.1 1.0 %copy-done.6 = f32[1,4,192,128]{3,2,1,0:T(8,128)S(1)} copy-done((f32[1,4,192,128]{3,2,1,0:T(8,128)S(1)}, f32[1,4,192,128]{3,2,1,0:T(8,128)}, u32[]{:S(2)}) %copy-start.6) | copy-done | bytes 393240
  9.1 0.7 copy-done.9
  9.7 0.7 copy-done.11
  10.4 0.7 copy-done.12
  11.0 1.3 %step0.1 = (f32[4,192,128]{2,1,0:T(8,128)S(1)}, f32[4,192,128]{2,1,0:T(8,128)S(1)}, f32[4,192,128]{2,1,0:T(8,128)S(1)}, f32[4,192,128]{2,1,0:T(8,128)S(1)}, f32[...) custom-call(f32[4,192,128]{2,1,0:T(8,128)S(1)} %bitcast.8, ...), custom_call_target="tpu_custom_call" | custom-call | flops 200000 | bytes 200000 | tf_op jit(solution)/shard_map/step0/pallas_call | solution.py:31
  12.3 0.4 collective-permute-done.2.a0
  12.8 0.0 collective-permute-done.3.b0
  12.8 1.3 %step1.1 = (f32[2,192,128]{2,1,0:T(8,128)S(1)}, f32[4,192,128]{2,1,0:T(8,128)S(1)}, f32[4,192,128]{2,1,0:T(8,128)S(1)}, f32[4,192,128]{2,1,0:T(8,128)S(1)}, f32[...) custom-call(f32[3,192,128]{2,1,0:T(8,128)S(1)} %collective-permute-done.2.a0, ...), custom_call_target="tpu_custom_call" | custom-call | flops 200000 | bytes 200000 | tf_op jit(solution)/shard_map/step1/pallas_call | solution.py:31
  14.1 0.2 collective-permute-start.4
  14.2 2.9 %collective-permute-start = (f32[2,192,128]{2,1,0:T(8,128)S(1)}, f32[2,192,128]{2,1,0:T(8,128)S(1)}, u32[]{:S(2)}, u32[]{:S(2)}) collective-permute-start(f32[2,192,128]{2,1,0:T(8,128)S(1)} %get-tuple-element.62), channel_id=1, source_target_pairs={{0,1},{1,0},{2,3},{3,2},{4,5},{5,4},{6,7},{7,6},{8,9},{9,8},{10,11... | collective-permute-start | bytes 589832 | tf_op jit(solution)/shard_map/ppermute | solution.py:184
  17.1 0.2 collective-permute-start.1
  17.2 0.0 collective-permute-done.4.other
  17.2 0.1 outer_scale.1
  17.3 5.2 %collective-permute-done.a1 = f32[2,192,128]{2,1,0:T(8,128)S(1)} collective-permute-done((f32[2,192,128]{2,1,0:T(8,128)S(1)}, f32[2,192,128]{2,1,0:T(8,128)S(1)}, u32[]{:S(2)}, u32[]{:S(2)}) %collective-permute-start) | collective-permute-done | bytes 196640 | tf_op jit(solution)/shard_map/ppermute | solution.py:184
  22.6 0.0 collective-permute-done.1.b1
  22.6 0.3 step2.1
  22.9 1.8 %collective-permute-start.7 = (f32[2,192,128]{2,1,0:T(8,128)S(1)}, f32[2,192,128]{2,1,0:T(8,128)S(1)}, u32[]{:S(2)}, u32[]{:S(2)}) collective-permute-start(f32[2,192,128]{2,1,0:T(8,128)S(1)} %get-tuple-element.84), channel_id=1, source_target_pairs={{0,1},{1,0},{2,3},{3,2},{4,5},{5,4},{6,7},{7,6},{8,9},{9,8},{10,11... | collective-permute-start | bytes 589832 | tf_op jit(solution)/shard_map/ppermute | solution.py:184
  24.7 0.0 collective-permute-start.8
  24.7 1.2 %step3.1 = (f32[4,192,128]{2,1,0:T(8,128)S(1)}, f32[4,192,128]{2,1,0:T(8,128)S(1)}, f32[2,192,128]{2,1,0:T(8,128)S(1)}, f32[2,192,128]{2,1,0:T(8,128)S(1)}) custom-call(f32[4,192,128]{2,1,0:T(8,128)S(1)} %get-tuple-element.78.field.pressure, f32[4,192,128]{2,1,0:T(8,128)S(1)} %get-tuple-element.79.before.pressure, ...), custom_call_target="tpu_custom_call" | custom-call | flops 200000 | bytes 200000 | tf_op jit(solution)/shard_map/step3/pallas_call | solution.py:31
  25.9 2.1 %collective-permute-start.5 = (f32[2,192,128]{2,1,0:T(8,128)S(1)}, f32[2,192,128]{2,1,0:T(8,128)S(1)}, u32[]{:S(2)}, u32[]{:S(2)}) collective-permute-start(f32[2,192,128]{2,1,0:T(8,128)S(1)} %get-tuple-element.82), channel_id=1, source_target_pairs={{0,1},{1,0},{2,3},{3,2},{4,5},{5,4},{6,7},{7,6},{8,9},{9,8},{10,11... | collective-permute-start | bytes 589832 | tf_op jit(solution)/shard_map/ppermute | solution.py:184
  27.9 0.0 collective-permute-start.6
  28.0 1.5 %receive.1 = (f32[4,192,128]{2,1,0:T(8,128)S(1)}, f32[4,192,128]{2,1,0:T(8,128)S(1)}, f32[4,192,128]{2,1,0:T(8,128)S(1)}, f32[4,192,128]{2,1,0:T(8,128)S(1)}, f32[4,192,128]{2,1,0:T(8,128)S(1)}) custom-call(s32[1,256]{1,0:T(1,128)S(1)} %bitcast.16, f32[4,256]{1,0:T(4,128)S(1)} %bitcast.15), custom_call_target="tpu_custom_call" | custom-call | flops 2000000 | bytes 2000000 | tf_op jit(solution)/shard_map/receive/pallas_call | solution.py:31
  29.5 0.7 collective-permute-done.7.a2
  30.1 0.0 collective-permute-done.8.b2
  30.1 1.3 %step4.1 = (f32[4,192,128]{2,1,0:T(8,128)S(1)}, f32[4,192,128]{2,1,0:T(8,128)S(1)}, f32[4,192,128]{2,1,0:T(8,128)S(1)}, f32[4,192,128]{2,1,0:T(8,128)S(1)}) custom-call(f32[2,192,128]{2,1,0:T(8,128)S(1)} %collective-permute-done.7.a2, f32[2,192,128]{2,1,0:T(8,128)S(1)} %collective-permute-done.8.b2, f32[4,192,128]{2,1,0:T(8,128)S(1)} %get-tuple-element.78.field.pressure, ...), custom_call_target="tpu_custom_call" | custom-call | flops 200000 | bytes 200000 | tf_op jit(solution)/shard_map/step4/pallas_call | solution.py:31
  31.5 2.3 %collective-permute-done.5.a3 = f32[2,192,128]{2,1,0:T(8,128)S(1)} collective-permute-done((f32[2,192,128]{2,1,0:T(8,128)S(1)}, f32[2,192,128]{2,1,0:T(8,128)S(1)}, u32[]{:S(2)}, u32[]{:S(2)}) %collective-permute-start.5) | collective-permute-done | bytes 196640 | tf_op jit(solution)/shard_map/ppermute | solution.py:184
  33.8 0.0 collective-permute-done.6.b3
  33.8 0.3 turn.1
  34.1 1.8 %collective-permute-start.11 = (f32[2,192,128]{2,1,0:T(8,128)S(1)}, f32[2,192,128]{2,1,0:T(8,128)S(1)}, u32[]{:S(2)}, u32[]{:S(2)}) collective-permute-start(f32[2,192,128]{2,1,0:T(8,128)S(1)} %get-tuple-element.99), channel_id=1, source_target_pairs={{0,1},{1,0},{2,3},{3,2},{4,5},{5,4},{6,7},{7,6},{8,9},{9,8},{10,11... | collective-permute-start | bytes 589832 | tf_op jit(solution)/shard_map/ppermute | solution.py:184
  35.9 0.6 adjoint3.1
  36.5 1.8 %collective-permute-start.9 = (f32[2,192,128]{2,1,0:T(8,128)S(1)}, f32[2,192,128]{2,1,0:T(8,128)S(1)}, u32[]{:S(2)}, u32[]{:S(2)}) collective-permute-start(f32[2,192,128]{2,1,0:T(8,128)S(1)} %get-tuple-element.97), channel_id=1, source_target_pairs={{0,1},{1,0},{2,3},{3,2},{4,5},{5,4},{6,7},{7,6},{8,9},{9,8},{10,11... | collective-permute-start | bytes 589832 | tf_op jit(solution)/shard_map/ppermute | solution.py:184
  38.4 0.0 collective-permute-start.10
  38.4 3.0 %collective-permute-done.11.a4 = f32[2,192,128]{2,1,0:T(8,128)S(1)} collective-permute-done((f32[2,192,128]{2,1,0:T(8,128)S(1)}, f32[2,192,128]{2,1,0:T(8,128)S(1)}, u32[]{:S(2)}, u32[]{:S(2)}) %collective-permute-start.11) | collective-permute-done | bytes 196640 | tf_op jit(solution)/shard_map/ppermute | solution.py:184
  41.4 1.3 %adjoint2.1 = (f32[4,192,128]{2,1,0:T(8,128)S(1)}, f32[4,192,128]{2,1,0:T(8,128)}, f32[4,192,128]{2,1,0:T(8,128)S(1)}, f32[4,192,128]{2,1,0:T(8,128)S(1)}, f32[4,192,128]{2,1,0:T(8,128)S(1)}) custom-call(f32[2,192,128]{2,1,0:T(8,128)S(1)} %collective-permute-done.11.a4, f32[2,192,128]{2,1,0:T(8,128)S(1)} %collective-permute-done.12.b4, ...), custom_call_target="tpu_custom_call" | custom-call | flops 200000 | bytes 200000 | tf_op jit(solution)/shard_map/adjoint2/pallas_call | solution.py:31
  42.7 2.1 %collective-permute-done.9.a5 = f32[2,192,128]{2,1,0:T(8,128)S(1)} collective-permute-done((f32[2,192,128]{2,1,0:T(8,128)S(1)}, f32[2,192,128]{2,1,0:T(8,128)S(1)}, u32[]{:S(2)}, u32[]{:S(2)}) %collective-permute-start.9) | collective-permute-done | bytes 196640 | tf_op jit(solution)/shard_map/ppermute | solution.py:184
  44.7 0.0 collective-permute-done.10.b5
  44.7 0.2 adjoint1.1
  45.0 1.9 %collective-permute-start.13 = (f32[2,192,128]{2,1,0:T(8,128)S(1)}, f32[2,192,128]{2,1,0:T(8,128)S(1)}, u32[]{:S(2)}, u32[]{:S(2)}) collective-permute-start(f32[2,192,128]{2,1,0:T(8,128)S(1)} %get-tuple-element.108), channel_id=1, source_target_pairs={{0,1},{1,0},{2,3},{3,2},{4,5},{5,4},{6,7},{7,6},{8,9},{9,8},{10,11... | collective-permute-start | bytes 589832 | tf_op jit(solution)/shard_map/ppermute | solution.py:184
  46.8 0.6 adjoint0.1.acc
  47.5 3.7 %collective-permute-done.13.a6 = f32[2,192,128]{2,1,0:T(8,128)S(1)} collective-permute-done((f32[2,192,128]{2,1,0:T(8,128)S(1)}, f32[2,192,128]{2,1,0:T(8,128)S(1)}, u32[]{:S(2)}, u32[]{:S(2)}) %collective-permute-start.13) | collective-permute-done | bytes 196640 | tf_op jit(solution)/shard_map/ppermute | solution.py:184
  51.1 0.0 collective-permute-done.14.b6
  51.1 0.1 finish.1
  51.3 0.0 copy-start.4
  51.3 0.1 collective-permute-start.15
  51.4 1.4 %collective-permute-done.15.y = f32[2,192,128]{2,1,0:T(8,128)S(1)} collective-permute-done((f32[2,192,128]{2,1,0:T(8,128)S(1)}, f32[2,192,128]{2,1,0:T(8,128)S(1)}, u32[]{:S(2)}, u32[]{:S(2)}) %collective-permute-start.15) | collective-permute-done | bytes 196640 | tf_op jit(solution)/shard_map/ppermute | solution.py:189
  52.8 1.6 %collective-permute-start.16 = (f32[2,192,128]{2,1,0:T(8,128)S(1)}, f32[2,192,128]{2,1,0:T(8,128)S(1)}, u32[]{:S(2)}, u32[]{:S(2)}) collective-permute-start(f32[2,192,128]{2,1,0:T(8,128)S(1)} %add.2.x), channel_id=1, source_target_pairs={{0,8},{4,12},{8,0},{12,4},{1,9},{5,13},{9,1},{13,5},{2,10},{6,14},... | collective-permute-start | bytes 589832 | tf_op jit(solution)/shard_map/ppermute | solution.py:189
  54.4 5.5 %collective-permute-done.16.y = f32[2,192,128]{2,1,0:T(8,128)S(1)} collective-permute-done((f32[2,192,128]{2,1,0:T(8,128)S(1)}, f32[2,192,128]{2,1,0:T(8,128)S(1)}, u32[]{:S(2)}, u32[]{:S(2)}) %collective-permute-start.16) | collective-permute-done | bytes 196640 | tf_op jit(solution)/shard_map/ppermute | solution.py:189
  59.9 0.1 collective-permute-start.17
  59.9 1.4 %collective-permute-done.17.other_ref = f32[2,192,128]{2,1,0:T(8,128)S(1)} collective-permute-done((f32[2,192,128]{2,1,0:T(8,128)S(1)}, f32[2,192,128]{2,1,0:T(8,128)S(1)}, u32[]{:S(2)}, u32[]{:S(2)}) %collective-permute-start.17) | collective-permute-done | bytes 196640 | tf_op jit(solution)/shard_map/ppermute | solution.py:189
  61.4 0.1 gather.1
  61.4 1.9 %collective-permute-start.18 = (f32[8,128]{1,0:T(8,128)S(1)}, f32[8,128]{1,0:T(8,128)S(1)}, u32[]{:S(2)}, u32[]{:S(2)}) collective-permute-start(f32[8,128]{1,0:T(8,128)S(1)} %get-tuple-element.121.refs_0_), channel_id=1, source_target_pairs={{0,1},{1,0},{2,3},{3,2},{4,5},{5,4},{6,7},{7,6},{8,9},{9,8},{10,11... | collective-permute-start | bytes 12296 | tf_op jit(solution)/shard_map/ppermute | solution.py:192
  63.3 1.2 %collective-permute-start.19 = (f32[8,128]{1,0:T(8,128)S(1)}, f32[8,128]{1,0:T(8,128)S(1)}, u32[]{:S(2)}, u32[]{:S(2)}) collective-permute-start(f32[8,128]{1,0:T(8,128)S(1)} %get-tuple-element.121.refs_0_), channel_id=1, source_target_pairs={{0,2},{1,3},{2,0},{3,1},{4,6},{5,7},{6,4},{7,5},{8,10},{9,11},{10,... | collective-permute-start | bytes 12296 | tf_op jit(solution)/shard_map/ppermute | solution.py:192
  64.5 1.4 %collective-permute-start.20 = (f32[8,128]{1,0:T(8,128)S(1)}, f32[8,128]{1,0:T(8,128)S(1)}, u32[]{:S(2)}, u32[]{:S(2)}) collective-permute-start(f32[8,128]{1,0:T(8,128)S(1)} %get-tuple-element.121.refs_0_), channel_id=1, source_target_pairs={{0,3},{1,2},{2,1},{3,0},{4,7},{5,6},{6,5},{7,4},{8,11},{9,10},{10,... | collective-permute-start | bytes 12296 | tf_op jit(solution)/shard_map/ppermute | solution.py:192
  65.9 0.0 collective-permute-done.18.refs_1_
  65.9 1.9 %collective-permute-done.19.refs_2_ = f32[8,128]{1,0:T(8,128)S(1)} collective-permute-done((f32[8,128]{1,0:T(8,128)S(1)}, f32[8,128]{1,0:T(8,128)S(1)}, u32[]{:S(2)}, u32[]{:S(2)}) %collective-permute-start.19) | collective-permute-done | bytes 4128 | tf_op jit(solution)/shard_map/ppermute | solution.py:192
  67.8 2.1 %collective-permute-done.20.refs_3_ = f32[8,128]{1,0:T(8,128)S(1)} collective-permute-done((f32[8,128]{1,0:T(8,128)S(1)}, f32[8,128]{1,0:T(8,128)S(1)}, u32[]{:S(2)}, u32[]{:S(2)}) %collective-permute-start.20) | collective-permute-done | bytes 4128 | tf_op jit(solution)/shard_map/ppermute | solution.py:192
  69.9 1.0 %update.1 = (f32[4,192,128]{2,1,0:T(8,128)}, f32[4,48,128]{2,1,0:T(8,128)}) custom-call(f32[4,192,128]{2,1,0:T(8,128)S(1)} %get-tuple-element.120.field, f32[4,192,128]{2,1,0:T(8,128)S(1)} %copy-done.4, f32[8,128]{1,0:T(8,128)S(1)} %get-tuple-element.121.refs_0_, f32[8,128]{1,0:T(8,128)S(1)} %collective-permute-done.18.refs_1_, ...), custom_call_target="tpu_custom_call" | custom-call | flops 200000 | bytes 200000 | tf_op jit(solution)/shard_map/update/pallas_call | solution.py:31
  (26 shorter events, 0.1 us)
Async XLA Ops:
  0.6 1.0 %copy-start = (f32[1,4,192,128]{3,2,1,0:T(8,128)S(1)}, f32[1,4,192,128]{3,2,1,0:T(8,128)}, u32[]{:S(2)}) copy-start(f32[1,4,192,128]{3,2,1,0:T(8,128)} %param.13) | copy-start | bytes 1179652
  1.6 1.0 %copy-start.2 = (f32[4,192,128]{2,1,0:T(8,128)S(1)}, f32[4,192,128]{2,1,0:T(8,128)}, u32[]{:S(2)}) copy-start(f32[4,192,128]{2,1,0:T(8,128)} %model.5) | copy-start | bytes 1179652
  2.7 10.1 %collective-permute-start.2 = (f32[3,192,128]{2,1,0:T(8,128)S(1)}, f32[3,192,128]{2,1,0:T(8,128)S(1)}, u32[]{:S(2)}, u32[]{:S(2)}) collective-permute-start(f32[3,192,128]{2,1,0:T(8,128)S(1)} %get-tuple-element.64), channel_id=1, source_target_pairs={{0,1},{1,0},{2,3},{3,2},{4,5},{5,4},{6,7},{7,6},{8,9},{9,8},{10,11... | collective-permute-start | bytes 884744 | tf_op jit(solution)/shard_map/ppermute | solution.py:184
  5.8 7.0 %collective-permute-start.3 = (f32[3,192,128]{2,1,0:T(8,128)S(1)}, f32[3,192,128]{2,1,0:T(8,128)S(1)}, u32[]{:S(2)}, u32[]{:S(2)}) collective-permute-start(f32[3,192,128]{2,1,0:T(8,128)S(1)} %get-tuple-element.65), channel_id=1, source_target_pairs={{0,4},{1,2},{2,1},{3,7},{4,0},{5,6},{6,5},{7,3},{8,12},{9,10},{10,... | collective-permute-start | bytes 884744 | tf_op jit(solution)/shard_map/ppermute | solution.py:184
  5.8 1.0 %copy-start.3 = (f32[4,192,128]{2,1,0:T(8,128)S(1)}, f32[4,192,128]{2,1,0:T(8,128)}, u32[]{:S(2)}) copy-start(f32[4,192,128]{2,1,0:T(8,128)} %model.5) | copy-start | bytes 1179652
  6.8 1.3 %copy-start.5 = (f32[1,3,4,192,128]{4,3,2,1,0:T(8,128)S(1)}, f32[1,3,4,192,128]{4,3,2,1,0:T(8,128)}, u32[]{:S(2)}) copy-start(f32[1,3,4,192,128]{4,3,2,1,0:T(8,128)} %param.14) | copy-start | bytes 3538948
  8.1 1.0 %copy-start.6 = (f32[1,4,192,128]{3,2,1,0:T(8,128)S(1)}, f32[1,4,192,128]{3,2,1,0:T(8,128)}, u32[]{:S(2)}) copy-start(f32[1,4,192,128]{3,2,1,0:T(8,128)} %param.12) | copy-start | bytes 1179652
  9.1 0.7 copy-start.9
  9.7 0.7 copy-start.11
  10.4 0.7 copy-start.12
  12.8 9.8 %copy-start.1 = (f32[1,4,192,128]{3,2,1,0:T(8,128)S(1)}, f32[1,4,192,128]{3,2,1,0:T(8,128)}, u32[]{:S(2)}) copy-start(f32[1,4,192,128]{3,2,1,0:T(8,128)} %param.13) | copy-start | bytes 1179652
  14.1 3.2 %collective-permute-start.4 = (f32[2,192,128]{2,1,0:T(8,128)S(1)}, f32[2,192,128]{2,1,0:T(8,128)S(1)}, u32[]{:S(2)}, u32[]{:S(2)}) collective-permute-start(f32[2,192,128]{2,1,0:T(8,128)S(1)} %get-tuple-element.74.mine), channel_id=1, source_target_pairs={{0,4},{4,0},{8,12},{12,8},{1,5},{5,1},{9,13},{13,9},{2,6},{6,2},{1... | collective-permute-start | bytes 589832 | tf_op jit(solution)/shard_map/ppermute | solution.py:189
  14.2 8.3 %collective-permute-start = (f32[2,192,128]{2,1,0:T(8,128)S(1)}, f32[2,192,128]{2,1,0:T(8,128)S(1)}, u32[]{:S(2)}, u32[]{:S(2)}) collective-permute-start(f32[2,192,128]{2,1,0:T(8,128)S(1)} %get-tuple-element.62), channel_id=1, source_target_pairs={{0,1},{1,0},{2,3},{3,2},{4,5},{5,4},{6,7},{7,6},{8,9},{9,8},{10,11... | collective-permute-start | bytes 589832 | tf_op jit(solution)/shard_map/ppermute | solution.py:184
  17.1 5.5 %collective-permute-start.1 = (f32[2,192,128]{2,1,0:T(8,128)S(1)}, f32[2,192,128]{2,1,0:T(8,128)S(1)}, u32[]{:S(2)}, u32[]{:S(2)}) collective-permute-start(f32[2,192,128]{2,1,0:T(8,128)S(1)} %get-tuple-element.63), channel_id=1, source_target_pairs={{0,4},{1,2},{2,1},{3,7},{4,0},{5,6},{6,5},{7,3},{8,12},{9,10},{10,... | collective-permute-start | bytes 589832 | tf_op jit(solution)/shard_map/ppermute | solution.py:184
  22.9 7.3 %collective-permute-start.7 = (f32[2,192,128]{2,1,0:T(8,128)S(1)}, f32[2,192,128]{2,1,0:T(8,128)S(1)}, u32[]{:S(2)}, u32[]{:S(2)}) collective-permute-start(f32[2,192,128]{2,1,0:T(8,128)S(1)} %get-tuple-element.84), channel_id=1, source_target_pairs={{0,1},{1,0},{2,3},{3,2},{4,5},{5,4},{6,7},{7,6},{8,9},{9,8},{10,11... | collective-permute-start | bytes 589832 | tf_op jit(solution)/shard_map/ppermute | solution.py:184
  24.7 5.5 %collective-permute-start.8 = (f32[2,192,128]{2,1,0:T(8,128)S(1)}, f32[2,192,128]{2,1,0:T(8,128)S(1)}, u32[]{:S(2)}, u32[]{:S(2)}) collective-permute-start(f32[2,192,128]{2,1,0:T(8,128)S(1)} %get-tuple-element.85), channel_id=1, source_target_pairs={{0,4},{1,2},{2,1},{3,7},{4,0},{5,6},{6,5},{7,3},{8,12},{9,10},{10,... | collective-permute-start | bytes 589832 | tf_op jit(solution)/shard_map/ppermute | solution.py:184
  24.7 3.3 %copy-start.13 = (f32[1,4,256]{2,1,0:T(4,128)S(1)}, f32[1,4,256]{2,1,0:T(4,128)}, u32[]{:S(2)}) copy-start(f32[1,4,256]{2,1,0:T(4,128)} %param.21) | copy-start | bytes 12292
  24.7 3.3 %copy-start.14 = (s32[256]{0:T(256)S(1)}, s32[256]{0:T(256)}, u32[]{:S(2)}) copy-start(s32[256]{0:T(256)} %param.20) | copy-start | bytes 3076
  24.7 5.5 %copy-start.10 = (f32[4]{0:T(128)S(1)}, f32[4]{0:T(128)}, u32[]{:S(2)}) copy-start(f32[4]{0:T(128)} %pulse.7) | copy-start | bytes 52
  25.9 7.9 %collective-permute-start.5 = (f32[2,192,128]{2,1,0:T(8,128)S(1)}, f32[2,192,128]{2,1,0:T(8,128)S(1)}, u32[]{:S(2)}, u32[]{:S(2)}) collective-permute-start(f32[2,192,128]{2,1,0:T(8,128)S(1)} %get-tuple-element.82), channel_id=1, source_target_pairs={{0,1},{1,0},{2,3},{3,2},{4,5},{5,4},{6,7},{7,6},{8,9},{9,8},{10,11... | collective-permute-start | bytes 589832 | tf_op jit(solution)/shard_map/ppermute | solution.py:184
  27.9 5.8 %collective-permute-start.6 = (f32[2,192,128]{2,1,0:T(8,128)S(1)}, f32[2,192,128]{2,1,0:T(8,128)S(1)}, u32[]{:S(2)}, u32[]{:S(2)}) collective-permute-start(f32[2,192,128]{2,1,0:T(8,128)S(1)} %get-tuple-element.83), channel_id=1, source_target_pairs={{0,4},{1,2},{2,1},{3,7},{4,0},{5,6},{6,5},{7,3},{8,12},{9,10},{10,... | collective-permute-start | bytes 589832 | tf_op jit(solution)/shard_map/ppermute | solution.py:184
  30.1 3.7 %copy-start.7 = (f32[1,4,192,128]{3,2,1,0:T(8,128)S(1)}, f32[1,4,192,128]{3,2,1,0:T(8,128)}, u32[]{:S(2)}) copy-start(f32[1,4,192,128]{3,2,1,0:T(8,128)} %param.15) | copy-start | bytes 1179652
  33.8 2.1 %copy-start.8 = (f32[1,4,192,128]{3,2,1,0:T(8,128)S(1)}, f32[1,4,192,128]{3,2,1,0:T(8,128)}, u32[]{:S(2)}) copy-start(f32[1,4,192,128]{3,2,1,0:T(8,128)} %param.16) | copy-start | bytes 1179652
  34.1 7.3 %collective-permute-start.11 = (f32[2,192,128]{2,1,0:T(8,128)S(1)}, f32[2,192,128]{2,1,0:T(8,128)S(1)}, u32[]{:S(2)}, u32[]{:S(2)}) collective-permute-start(f32[2,192,128]{2,1,0:T(8,128)S(1)} %get-tuple-element.99), channel_id=1, source_target_pairs={{0,1},{1,0},{2,3},{3,2},{4,5},{5,4},{6,7},{7,6},{8,9},{9,8},{10,11... | collective-permute-start | bytes 589832 | tf_op jit(solution)/shard_map/ppermute | solution.py:184
  35.9 5.5 %collective-permute-start.12 = (f32[2,192,128]{2,1,0:T(8,128)S(1)}, f32[2,192,128]{2,1,0:T(8,128)S(1)}, u32[]{:S(2)}, u32[]{:S(2)}) collective-permute-start(f32[2,192,128]{2,1,0:T(8,128)S(1)} %get-tuple-element.100), channel_id=1, source_target_pairs={{0,4},{1,2},{2,1},{3,7},{4,0},{5,6},{6,5},{7,3},{8,12},{9,10},{10,... | collective-permute-start | bytes 589832 | tf_op jit(solution)/shard_map/ppermute | solution.py:184
  36.5 8.2 %collective-permute-start.9 = (f32[2,192,128]{2,1,0:T(8,128)S(1)}, f32[2,192,128]{2,1,0:T(8,128)S(1)}, u32[]{:S(2)}, u32[]{:S(2)}) collective-permute-start(f32[2,192,128]{2,1,0:T(8,128)S(1)} %get-tuple-element.97), channel_id=1, source_target_pairs={{0,1},{1,0},{2,3},{3,2},{4,5},{5,4},{6,7},{7,6},{8,9},{9,8},{10,11... | collective-permute-start | bytes 589832 | tf_op jit(solution)/shard_map/ppermute | solution.py:184
  38.4 6.4 %collective-permute-start.10 = (f32[2,192,128]{2,1,0:T(8,128)S(1)}, f32[2,192,128]{2,1,0:T(8,128)S(1)}, u32[]{:S(2)}, u32[]{:S(2)}) collective-permute-start(f32[2,192,128]{2,1,0:T(8,128)S(1)} %get-tuple-element.98), channel_id=1, source_target_pairs={{0,4},{1,2},{2,1},{3,7},{4,0},{5,6},{6,5},{7,3},{8,12},{9,10},{10,... | collective-permute-start | bytes 589832 | tf_op jit(solution)/shard_map/ppermute | solution.py:184
  45.0 6.2 %collective-permute-start.13 = (f32[2,192,128]{2,1,0:T(8,128)S(1)}, f32[2,192,128]{2,1,0:T(8,128)S(1)}, u32[]{:S(2)}, u32[]{:S(2)}) collective-permute-start(f32[2,192,128]{2,1,0:T(8,128)S(1)} %get-tuple-element.108), channel_id=1, source_target_pairs={{0,1},{1,0},{2,3},{3,2},{4,5},{5,4},{6,7},{7,6},{8,9},{9,8},{10,11... | collective-permute-start | bytes 589832 | tf_op jit(solution)/shard_map/ppermute | solution.py:184
  46.8 4.3 %collective-permute-start.14 = (f32[2,192,128]{2,1,0:T(8,128)S(1)}, f32[2,192,128]{2,1,0:T(8,128)S(1)}, u32[]{:S(2)}, u32[]{:S(2)}) collective-permute-start(f32[2,192,128]{2,1,0:T(8,128)S(1)} %get-tuple-element.109), channel_id=1, source_target_pairs={{0,4},{1,2},{2,1},{3,7},{4,0},{5,6},{6,5},{7,3},{8,12},{9,10},{10,... | collective-permute-start | bytes 589832 | tf_op jit(solution)/shard_map/ppermute | solution.py:184
  51.3 18.6 %copy-start.4 = (f32[4,192,128]{2,1,0:T(8,128)S(1)}, f32[4,192,128]{2,1,0:T(8,128)}, u32[]{:S(2)}) copy-start(f32[4,192,128]{2,1,0:T(8,128)} %model.5) | copy-start | bytes 1179652
  51.3 1.5 %collective-permute-start.15 = (f32[2,192,128]{2,1,0:T(8,128)S(1)}, f32[2,192,128]{2,1,0:T(8,128)S(1)}, u32[]{:S(2)}, u32[]{:S(2)}) collective-permute-start(f32[2,192,128]{2,1,0:T(8,128)S(1)} %get-tuple-element.119), channel_id=1, source_target_pairs={{0,4},{4,0},{8,12},{12,8},{1,5},{5,1},{9,13},{13,9},{2,6},{6,2},{1... | collective-permute-start | bytes 589832 | tf_op jit(solution)/shard_map/ppermute | solution.py:189
  52.8 7.0 %collective-permute-start.16 = (f32[2,192,128]{2,1,0:T(8,128)S(1)}, f32[2,192,128]{2,1,0:T(8,128)S(1)}, u32[]{:S(2)}, u32[]{:S(2)}) collective-permute-start(f32[2,192,128]{2,1,0:T(8,128)S(1)} %add.2.x), channel_id=1, source_target_pairs={{0,8},{4,12},{8,0},{12,4},{1,9},{5,13},{9,1},{13,5},{2,10},{6,14},... | collective-permute-start | bytes 589832 | tf_op jit(solution)/shard_map/ppermute | solution.py:189
  59.9 1.5 %collective-permute-start.17 = (f32[2,192,128]{2,1,0:T(8,128)S(1)}, f32[2,192,128]{2,1,0:T(8,128)S(1)}, u32[]{:S(2)}, u32[]{:S(2)}) collective-permute-start(f32[2,192,128]{2,1,0:T(8,128)S(1)} %add.3.mine_ref), channel_id=1, source_target_pairs={{0,4},{4,0},{8,12},{12,8},{1,5},{5,1},{9,13},{13,9},{2,6},{6,2},{1... | collective-permute-start | bytes 589832 | tf_op jit(solution)/shard_map/ppermute | solution.py:189
  61.4 4.5 %collective-permute-start.18 = (f32[8,128]{1,0:T(8,128)S(1)}, f32[8,128]{1,0:T(8,128)S(1)}, u32[]{:S(2)}, u32[]{:S(2)}) collective-permute-start(f32[8,128]{1,0:T(8,128)S(1)} %get-tuple-element.121.refs_0_), channel_id=1, source_target_pairs={{0,1},{1,0},{2,3},{3,2},{4,5},{5,4},{6,7},{7,6},{8,9},{9,8},{10,11... | collective-permute-start | bytes 12296 | tf_op jit(solution)/shard_map/ppermute | solution.py:192
  63.3 4.5 %collective-permute-start.19 = (f32[8,128]{1,0:T(8,128)S(1)}, f32[8,128]{1,0:T(8,128)S(1)}, u32[]{:S(2)}, u32[]{:S(2)}) collective-permute-start(f32[8,128]{1,0:T(8,128)S(1)} %get-tuple-element.121.refs_0_), channel_id=1, source_target_pairs={{0,2},{1,3},{2,0},{3,1},{4,6},{5,7},{6,4},{7,5},{8,10},{9,11},{10,... | collective-permute-start | bytes 12296 | tf_op jit(solution)/shard_map/ppermute | solution.py:192
  64.5 5.4 %collective-permute-start.20 = (f32[8,128]{1,0:T(8,128)S(1)}, f32[8,128]{1,0:T(8,128)S(1)}, u32[]{:S(2)}, u32[]{:S(2)}) collective-permute-start(f32[8,128]{1,0:T(8,128)S(1)} %get-tuple-element.121.refs_0_), channel_id=1, source_target_pairs={{0,3},{1,2},{2,1},{3,0},{4,7},{5,6},{6,5},{7,4},{8,11},{9,10},{10,... | collective-permute-start | bytes 12296 | tf_op jit(solution)/shard_map/ppermute | solution.py:192

commit v2 on v1

--- a/solution.py
+++ b/solution.py
@@ -4,6 +4,7 @@
 from jax.experimental import pallas as pl
 from jax.experimental.pallas import tpu as pltpu
 from jax.sharding import PartitionSpec as P
+
 
 STEPS = 4
 
@@ -23,14 +24,18 @@
 PAD = 8
 VMEM_SPEC = pl.BlockSpec(memory_space=pltpu.VMEM)
 SMEM_SPEC = pl.BlockSpec(memory_space=pltpu.SMEM)
+HBM_SPEC = pl.BlockSpec(memory_space=pltpu.HBM)
 F32 = jnp.float32
 
 
-def run(kernel, name, outs, args, scratch=(), smem=(), cost=200_000):
-    specs = [SMEM_SPEC if i in smem else VMEM_SPEC for i in range(len(args))]
+def run(kernel, outs, args, scratch=(), hbm=(), cost=200_000):
+    specs = [HBM_SPEC if i in hbm else VMEM_SPEC for i in range(len(args))]
+    args = [
+        pltpu.with_memory_space_constraint(arg, pltpu.HBM) if i in hbm else arg
+        for i, arg in enumerate(args)
+    ]
     return pl.pallas_call(
         kernel,
-        name=name,
         out_shape=[jax.ShapeDtypeStruct(shape, F32) for shape in outs],
         in_specs=specs,
         out_specs=[VMEM_SPEC] * len(outs),
@@ -181,9 +186,9 @@
                 pairs_b.append((s * slabs + k, (s ^ 1) * slabs + k))
 
     def exchange(sends):
-        return lax.ppermute(sends[0], "slab", pairs_a), lax.ppermute(
-            sends[1], ("shot", "slab"), pairs_b
-        )
+        got_a = lax.ppermute(sends[0], "slab", pairs_a)
+        got_b = lax.ppermute(sends[1], ("shot", "slab"), pairs_b)
+        return got_a, got_b
 
     def shot_swap(value, bit):
         return lax.ppermute(value, "shot", [(i, i ^ bit) for i in range(shots)])
@@ -191,29 +196,58 @@
     def slab_swap(value, bit):
         return lax.ppermute(value, "slab", [(i, i ^ bit) for i in range(slabs)])
 
-    def first_sends(field, model, a, b):
-        send_planes(a, b, field)
+    def first_sends(field, model, a, b, arrived):
         odd = lax.rem(lax.axis_index("slab"), 2)
         mine = lax.rem(lax.axis_index("shot"), 2)
         top = depth - 2
-        a[2] = model[top * (1 - odd) + mine]
-        b[2] = model[top * odd + mine]
-
-    got_now = exchange(run(first_sends, "sends0", [(3, width, lanes)] * 2, (now, slowness)))
-
-    def step0(field, before, variables, model, cells, signs, pulse, *outs):
-        lap, newer, scaled, factor, source, rest0, rest1, rest2, rest3, a, b, pad = outs
-        rests = (rest0, rest1, rest2, rest3)
+        copies = []
+        for k, (out, first) in enumerate(((a, top * (1 - odd)), (b, top * odd))):
+            copies.append(
+                pltpu.make_async_copy(field.at[pl.ds(first, 2)], out.at[0:2], arrived.at[2 * k])
+            )
+            copies.append(
+                pltpu.make_async_copy(model.at[first + mine], out.at[2], arrived.at[2 * k + 1])
+            )
+        for copy in copies:
+            copy.start()
+        for copy in copies:
+            copy.wait()
+
+    got0 = exchange(
+        run(
+            first_sends,
+            [(3, width, lanes)] * 2,
+            (now, slowness),
+            [pltpu.SemaphoreType.DMA((4,))],
+            hbm=(0, 1),
+        ),
+    )
+
+    def step0(*refs):
+        sources, refs = refs[:7], refs[7:]
+        field, model, lap, newer, scaled, factor = refs[:6]
+        pushes, rests, (a, b), refs = refs[6:9], refs[9:13], refs[13:15], refs[15:]
+        before, variables, cells, signs, pulse, source, pad, arrived = refs
+        targets = (field, cells, signs, pulse, model, variables, before)
+        copies = [
+            pltpu.make_async_copy(src, dst, arrived.at[i])
+            for i, (src, dst) in enumerate(zip(sources, targets))
+        ]
+        for copy in copies:
+            copy.start()
         clear_pads(pad)
-        for p in planes:
-            pad[p, PAD : PAD + width] = field[p]
         first_row = lax.axis_index("slab") * (depth * width)
+        for copy in copies[:4]:
+            copy.wait()
         columns = jnp.where(is_lane(cells[...], lanes), signs[...].astype(F32), 0.0)
         columns = columns.astype(jnp.bfloat16)
         for p in planes:
             source[p] = spread(
                 one_hot_rows(cells[...], first_row + p * width, width, lanes), columns
             )
+            pad[p, PAD : PAD + width] = field[p]
+        for copy in copies[4:]:
+            copy.wait()
         for p in planes:
             for r, n in rows:
                 at = (p, slice(r, r + n))
@@ -230,23 +264,35 @@
                     rests[n_step][at] = sum(terms[1:], terms[0])
                 curved = own_laplace(pad, p, r, n)
                 lap[at] = curved
+                shape = source[at]
                 newer[at] = (
                     2.0 * field[at]
                     - before[at]
                     + scale * (curved + rests[0][at])
-                    + pulse[0] * source[at]
+                    + pulse[0] * shape
                 )
+                for n_step in range(1, STEPS):
+                    pushes[n_step - 1][at] = pulse[n_step] * shape
         send_planes(a, b, newer)
 
-    lap0s, p1s, scaled, factor, source, rest0, rest1, rest2, rest3, *sends = run(
+    now, model, lap0s, p1s, scaled, factor, *fields = run(
         step0,
-        "step0",
-        [whole] * 9 + [pair] * 2,
-        (now, older, relax, slowness, src_cells, src_signs, wavelet),
-        [padded],
-        smem=(6,),
-    )
-    got_p1 = exchange(sends)
+        [whole] * 13 + [pair] * 2,
+        (now, src_cells, src_signs, wavelet, slowness, relax, older),
+        [
+            pltpu.VMEM(whole, F32),
+            pltpu.VMEM(relax.shape, F32),
+            pltpu.VMEM(src_cells.shape, jnp.int32),
+            pltpu.VMEM(src_signs.shape, jnp.int32),
+            pltpu.SMEM(wavelet.shape, F32),
+            pltpu.VMEM(whole, F32),
+            padded,
+            pltpu.SemaphoreType.DMA((7,)),
+        ],
+        hbm=range(7),
+    )
+    (push1, push2, push3), (rest0, rest1, rest2, rest3), sends = fields[:3], fields[3:7], fields[7:]
+    got1 = exchange(sends)
 
     def receive(cells, values, *outs):
         first_row = lax.axis_index("slab") * (depth * width)
@@ -263,21 +309,26 @@
             outs[0][p] = spread(hot, columns[0])
             for level in range(STEPS):
                 first = 1 + 3 * level
-                outs[1 + level][p] = (
+                outs[3 + level][p] = (
                     spread(hot, columns[first + 2]) + spread(hot, columns[first + 1])
                 ) + spread(hot, columns[first])
-
-    counts, seen0, seen1, seen2, seen3 = run(
-        receive, "receive", [whole] * 5, (receivers, seen), cost=2_000_000
-    )
-
-    def step1(a0, b0, field, lap_s, newer_s, scale, rest, rest_next, src, pulse, *outs):
-        model_ghosts, lap, accel, newer, lap_next, newest, pad = outs
+        for j in range(2):
+            for out, p in ((outs[1], j - 2), (outs[2], depth + j)):
+                hot = one_hot_rows(cells[...], first_row + p * width, width, lanes)
+                out[j] = spread(hot, columns[0])
+
+    counts, counts_low, counts_high, seen0, seen1, seen2, seen3 = run(
+        receive, [whole] + [pair] * 2 + [whole] * STEPS, (receivers, seen), cost=2_000_000
+    )
+
+    def forward1(a, b, field, lap_s, newer_s, scale, rest, rest_next, push, ready, *outs):
+        del ready
+        model_ghosts, lap, accel, newer, lap_next, newest, out_a, out_b, pad = outs
         clear_pads(pad)
-        model_ghosts[0] = a0[2]
-        model_ghosts[1] = b0[2]
+        model_ghosts[0] = a[2]
+        model_ghosts[1] = b[2]
         for r, n in rows:
-            low, high = ghosts(a0, b0, r, n)
+            low, high = ghosts(a, b, r, n)
             for p in planes:
                 at = (p, slice(r, r + n))
                 outside = reach(low, high, p, depth)
@@ -296,20 +347,20 @@
                     2.0 * newer[at]
                     - field[at]
                     + scale[at] * (curved + (rest_next[at] - echo[0] * lap[at]))
-                    + pulse[1] * src[at]
+                    + push[at]
                 )
-
-    model_ghosts, lap0, accel0, p1, lap1s, p2s = run(
-        step1,
-        "step1",
-        [pair] + [whole] * 5,
-        (*got_now, now, lap0s, p1s, scaled, rest0, rest1, source, wavelet),
+        send_planes(out_a, out_b, newest)
+
+    model_ghosts, lap0, accel0, p1, lap1s, p2s, *sends = run(
+        forward1,
+        [pair] + [whole] * 5 + [pair] * 2,
+        (*got0, now, lap0s, p1s, scaled, rest0, rest1, push1, counts_low),
         [padded],
-        smem=(9,),
-    )
+    )
+    got2 = exchange(sends)
     partner_ghosts = shot_swap(model_ghosts, 1)
 
-    def outer_scale(mine, other, low, high):
+    def outer_scale(mine, other, hits_low, hits_high, low, high, turn_low, turn_high):
         slab, count = lax.axis_index("slab"), lax.axis_size("slab")
         even = lax.rem(slab, 2) == 0
         first = lax.rem(lax.axis_index("shot"), 2) == 0
@@ -319,154 +370,224 @@
                 have = first if j == 0 else jnp.logical_not(first)
                 from_a = jnp.where(have, mine[0, at], other[0, at])
                 from_b = jnp.where(have, mine[1, at], other[1, at])
-                for side, ref, at_end in (
-                    (jnp.where(even, from_b, from_a), low, slab == 0),
-                    (jnp.where(even, from_a, from_b), high, slab == count - 1),
+                for side, ref, turn, hits, at_end in (
+                    (jnp.where(even, from_b, from_a), low, turn_low, hits_low, slab == 0),
+                    (jnp.where(even, from_a, from_b), high, turn_high, hits_high, slab == count - 1),
                 ):
                     value = courant / (side * side)
-                    ref[j, at] = jnp.where(at_end, jnp.zeros_like(value), value)
-
-    scale_low, scale_high = run(
-        outer_scale, "outer_scale", [pair] * 2, (model_ghosts, partner_ghosts)
-    )
-
-    def step2(a1, b1, field, lap_s, newer_s, scale, s_low, s_high, rest, lap_old, *outs):
-        lap, accel, newer, a, b = outs
+                    value = jnp.where(at_end, jnp.zeros_like(value), value)
+                    ref[j, at] = value
+                    turn[j, at] = value * value * hits[j, at]
+
+    scale_low, scale_high, turn_low, turn_high = run(
+        outer_scale, [pair] * 4, (model_ghosts, partner_ghosts, counts_low, counts_high)
+    )
+
+    def forward2(
+        a, b, older_, s_low, s_high, lap_s, newer_s, scale, rest, lap_old, field, rest_next, push, *outs
+    ):
+        lap, accel, newer, accel_s, newest, out_a, out_b, pad = outs
+        clear_pads(pad)
         for r, n in rows:
-            low, high = ghosts(a1, b1, r, n)
-            low, high = complete(low, high, s_low, s_high, field, r, n)
+            low, high = ghosts(a, b, r, n)
+            low, high = complete(low, high, s_low, s_high, older_, r, n)
             for p in planes:
                 at = (p, slice(r, r + n))
                 outside = reach(low, high, p, depth)
                 curved = lap_s[at] + outside
                 lap[at] = curved
                 accel[at] = curved + (rest[at] - echo[0] * lap_old[at])
-                newer[at] = newer_s[at] + scale[at] * outside
-        send_planes(a, b, newer)
-
-    lap1, accel1, p2, *sends = run(
-        step2,
-        "step2",
-        [whole] * 3 + [pair] * 2,
-        (*got_p1, now, lap1s, p2s, scaled, scale_low, scale_high, rest1, lap0),
-    )
-    got_p2 = exchange(sends)
-
-    def step3(field, before, scale, rest, lap_a, lap_b, src, pulse, *outs):
-        accel_s, newer, a, b, pad = outs
-        clear_pads(pad)
-        for p in planes:
-            pad[p, PAD : PAD + width] = field[p]
-        for p in planes:
-            for r, n in rows:
-                at = (p, slice(r, r + n))
-                part = rest[at] - echo[0] * lap_b[at] - echo[1] * lap_a[at]
-                accel = own_laplace(pad, p, r, n) + part
-                accel_s[at] = accel
-                newer[at] = (
-                    2.0 * field[at] - before[at] + scale[at] * accel + pulse[2] * src[at]
-                )
-        send_planes(a, b, newer)
-
-    accel2s, p3s, *sends = run(
-        step3,
-        "step3",
-        [whole] * 2 + [pair] * 2,
-        (p2, p1, scaled, rest2, lap0, lap1, source, wavelet),
-        [padded],
-        smem=(7,),
-    )
-    got_p3 = exchange(sends)
-
-    def step4(a2, b2, field, accel_s, newer_s, scale, rest2_, rest3_, lap_a, lap_b, src, pulse, *outs):
-        accel, newer, accel_next, newest, pad = outs
-        clear_pads(pad)
-        for r, n in rows:
-            low, high = ghosts(a2, b2, r, n)
-            for p in planes:
-                at = (p, slice(r, r + n))
-                outside = reach(low, high, p, depth)
-                accel[at] = accel_s[at] + outside
                 value = newer_s[at] + scale[at] * outside
                 newer[at] = value
                 pad[p, PAD + r : PAD + r + n] = value
         for p in planes:
             for r, n in rows:
                 at = (p, slice(r, r + n))
+                part = rest_next[at] - echo[0] * lap[at] - echo[1] * lap_old[at]
+                acc = own_laplace(pad, p, r, n) + part
+                accel_s[at] = acc
+                newest[at] = 2.0 * newer[at] - field[at] + scale[at] * acc + push[at]
+        send_planes(out_a, out_b, newest)
+
+    lap1, accel1, p2, accel2s, p3s, *sends = run(
+        forward2,
+        [whole] * 5 + [pair] * 2,
+        (
+            *got1,
+            now,
+            scale_low,
+            scale_high,
+            lap1s,
+            p2s,
+            scaled,
+            rest1,
+            lap0,
+            p1,
+            rest2,
+            push2,
+        ),
+        [padded],
+    )
+    got3 = exchange(sends)
+
+    def forward3(
+        a,
+        b,
+        older_,
+        s_low,
+        s_high,
+        accel_old,
+        newer_s,
+        scale,
+        rest2_,
+        rest3_,
+        lap_a,
+        lap_b,
+        field,
+        push,
+        hits,
+        sums,
+        back,
+        *outs,
+    ):
+        accel, newer, accel_s, united_s, drive_s, out_a, out_b, pad = outs
+        clear_pads(pad)
+        for r, n in rows:
+            low, high = ghosts(a, b, r, n)
+            low, high = complete(low, high, s_low, s_high, older_, r, n)
+            for p in planes:
+                at = (p, slice(r, r + n))
+                outside = reach(low, high, p, depth)
+                accel[at] = accel_old[at] + outside
+                value = newer_s[at] + scale[at] * outside
+                newer[at] = value
+                pad[p, PAD + r : PAD + r + n] = value
+        for p in planes:
+            for r, n in rows:
+                at = (p, slice(r, r + n))
                 lap_c = accel[at] - (rest2_[at] - echo[0] * lap_b[at] - echo[1] * lap_a[at])
                 part = rest3_[at] - echo[0] * lap_c - echo[1] * lap_b[at] - echo[2] * lap_a[at]
                 acc = own_laplace(pad, p, r, n) + part
-                accel_next[at] = acc
-                newest[at] = (
-                    2.0 * newer[at] - field[at] + scale[at] * acc + pulse[3] * src[at]
-                )
-
-    accel2, p3, accel3s, p4s = run(
-        step4,
-        "step4",
-        [whole] * 4,
-        (*got_p2, p2, accel2s, p3s, scaled, rest2, rest3, lap0, lap1, source, wavelet),
+                accel_s[at] = acc
+                newest = 2.0 * newer[at] - field[at] + scale[at] * acc + push[at]
+                value = back[at] + (hits[at] * newest - sums[at])
+                united_s[at] = value
+                drive_s[at] = scale[at] * value
+        send_planes(out_a, out_b, drive_s)
+
+    accel2, p3, accel3s, united3s, drive3s, *sends = run(
+        forward3,
+        [whole] * 5 + [pair] * 2,
+        (
+            *got2,
+            p1,
+            scale_low,
+            scale_high,
+            accel2s,
+            p3s,
+            scaled,
+            rest2,
+            rest3,
+            lap0,
+            lap1,
+            p2,
+            push3,
+            counts,
+            seen3,
+            back_now,
+        ),
         [padded],
-        smem=(11,),
-    )
-
-    def turn(a3, b3, field, accel_s, newer_s, scale, s_low, s_high, hits, sums, back, *outs):
-        united, drive, total, a, b = outs
+    )
+    got4 = exchange(sends)
+
+    def forward4(
+        a,
+        b,
+        older_,
+        s_low,
+        s_high,
+        accel_old,
+        united_old,
+        drive_old,
+        scale,
+        hits,
+        back,
+        pressure,
+        sums,
+        *outs,
+    ):
+        united, drive, total, united_s, drive_s, out_a, out_b, pad = outs
+        clear_pads(pad)
         for r, n in rows:
-            low, high = ghosts(a3, b3, r, n)
-            low, high = complete(low, high, s_low, s_high, field, r, n)
+            low, high = ghosts(a, b, r, n)
+            low, high = complete(low, high, s_low, s_high, older_, r, n)
             for p in planes:
                 at = (p, slice(r, r + n))
                 outside = reach(low, high, p, depth)
-                newest = newer_s[at] + scale[at] * outside
-                value = back[at] + (hits[at] * newest - sums[at])
+                change = hits[at] * (scale[at] * outside)
+                value = united_old[at] + change
                 united[at] = value
-                drive[at] = scale[at] * value
-                total[at] = value * (accel_s[at] + outside)
-        send_planes(a, b, drive)
-
-    united3, drive3, accum, *sends = run(
-        turn,
-        "turn",
-        [whole] * 3 + [pair] * 2,
-        (*got_p3, p2, accel3s, p4s, scaled, scale_low, scale_high, counts, seen3, back_now),
-    )
-    got_d3 = exchange(sends)
-
-    def adjoint3(field, drive, back, scale, hits, pressure, sums, *outs):
-        united, drive_next, a, b, pad = outs
-        clear_pads(pad)
-        for p in planes:
-            pad[p, PAD : PAD + width] = drive[p]
+                total[at] = value * (accel_old[at] + outside)
+                pushed = drive_old[at] + scale[at] * change
+                drive[at] = pushed
+                pad[p, PAD + r : PAD + r + n] = pushed
         for p in planes:
             for r, n in rows:
                 at = (p, slice(r, r + n))
                 value = (
                     back[at]
-                    + 2.0 * field[at]
+                    + 2.0 * united[at]
                     + own_laplace(pad, p, r, n)
                     + (hits[at] * pressure[at] - sums[at])
                 )
-                united[at] = value
-                drive_next[at] = scale[at] * value - echo[0] * drive[at]
-        send_planes(a, b, drive_next)
-
-    united2s, drive2s, *sends = run(
-        adjoint3,
-        "adjoint3",
-        [whole] * 2 + [pair] * 2,
-        (united3, drive3, back_prev, scaled, counts, p3, seen2),
+                united_s[at] = value
+                drive_s[at] = scale[at] * value - echo[0] * drive[at]
+        send_planes(out_a, out_b, drive_s)
+
+    united3, drive3, accum, united2s, drive2s, *sends = run(
+        forward4,
+        [whole] * 5 + [pair] * 2,
+        (
+            *got3,
+            p2,
+            scale_low,
+            scale_high,
+            accel3s,
+            united3s,
+            drive3s,
+            scaled,
+            counts,
+            back_prev,
+            p3,
+            seen2,
+        ),
         [padded],
     )
-    got_d2 = exchange(sends)
+    got5 = exchange(sends)
 
     def adjoint2(
-        a4, b4, united_s, drive_s, scale, drive_old, united_old, hits, pressure, sums, accel, acc, *outs
+        a,
+        b,
+        older_,
+        s_low,
+        s_high,
+        united_s,
+        drive_s,
+        scale,
+        drive_old,
+        united_old,
+        hits,
+        pressure,
+        sums,
+        accel,
+        acc,
+        *outs,
     ):
-        united, drive, total, united_next, drive_next, pad = outs
+        united, drive, total, united_next, drive_next, out_a, out_b, pad = outs
         clear_pads(pad)
         for r, n in rows:
-            low, high = ghosts(a4, b4, r, n)
+            low, high = ghosts(a, b, r, n)
+            low, high = complete(low, high, s_low, s_high, older_, r, n)
             for p in planes:
                 at = (p, slice(r, r + n))
                 outside = reach(low, high, p, depth)
@@ -489,13 +610,16 @@
                 drive_next[at] = (
                     scale[at] * (value - echo[0] * united[at]) - echo[1] * drive_old[at]
                 )
-
-    united2, drive2, accum, united1s, drive1s = run(
+        send_planes(out_a, out_b, drive_next)
+
+    united2, drive2, accum, united1s, drive1s, *sends = run(
         adjoint2,
-        "adjoint2",
-        [whole] * 5,
+        [whole] * 5 + [pair] * 2,
         (
-            *got_d3,
+            *got4,
+            p3,
+            turn_low,
+            turn_high,
             united2s,
             drive2s,
             scaled,
@@ -509,32 +633,37 @@
         ),
         [padded],
     )
-
-    def adjoint1(a5, b5, drive_old, united_s, drive_s, scale, s_low, s_high, *outs):
-        united, drive, a, b = outs
+    got6 = exchange(sends)
+
+    def adjoint1(
+        a,
+        b,
+        older_,
+        s_low,
+        s_high,
+        united_s,
+        drive_s,
+        scale,
+        united_old,
+        hits,
+        pressure,
+        sums,
+        accel_b,
+        accel_a,
+        acc,
+        total,
+        united,
+        pad,
+    ):
+        clear_pads(pad)
         for r, n in rows:
-            low, high = ghosts(a5, b5, r, n)
-            low, high = complete(low, high, s_low, s_high, drive_old, r, n)
+            low, high = ghosts(a, b, r, n)
+            low, high = complete(low, high, s_low, s_high, older_, r, n)
             for p in planes:
                 at = (p, slice(r, r + n))
                 outside = reach(low, high, p, depth)
                 united[at] = united_s[at] + outside
-                drive[at] = drive_s[at] + scale[at] * outside
-        send_planes(a, b, drive)
-
-    united1, drive1, *sends = run(
-        adjoint1,
-        "adjoint1",
-        [whole] * 2 + [pair] * 2,
-        (*got_d2, drive3, united1s, drive1s, scaled, scale_low, scale_high),
-    )
-    got_d1 = exchange(sends)
-
-    def adjoint0(drive, united, united_old, hits, pressure, sums, accel_b, accel_a, acc, *outs):
-        total, pad = outs
-        clear_pads(pad)
-        for p in planes:
-            pad[p, PAD : PAD + width] = drive[p]
+                pad[p, PAD + r : PAD + r + n] = drive_s[at] + scale[at] * outside
         for p in planes:
             for r, n in rows:
                 at = (p, slice(r, r + n))
@@ -547,17 +676,32 @@
                 total[at] = acc[at] + united[at] * accel_b[at] + value * accel_a[at]
 
     (accum,) = run(
-        adjoint0,
-        "adjoint0",
+        adjoint1,
         [whole],
-        (drive1, united1, united2, counts, p1, seen0, accel1, accel0, accum),
-        [padded],
-    )
-
-    def finish(a6, b6, acc, accel, fact, keep, send, grad):
+        (
+            *got5,
+            drive3,
+            scale_low,
+            scale_high,
+            united1s,
+            drive1s,
+            scaled,
+            united2,
+            counts,
+            p1,
+            seen0,
+            accel1,
+            accel0,
+            accum,
+        ),
+        [pltpu.VMEM(whole, F32), padded],
+    )
+
+    def finish(a, b, older_, s_low, s_high, acc, accel, fact, keep, send, grad):
         mine = lax.rem(lax.axis_index("shot"), 2)
         for r, n in rows:
-            low, high = ghosts(a6, b6, r, n)
+            low, high = ghosts(a, b, r, n)
+            low, high = complete(low, high, s_low, s_high, older_, r, n)
             for p in planes:
                 at = (p, slice(r, r + n))
                 outside = reach(low, high, p, depth)
@@ -568,19 +712,18 @@
 
     keep, give = run(
         finish,
-        "finish",
         [half] * 2,
-        (*got_d1, accum, accel0, factor),
+        (*got6, drive2, scale_low, scale_high, accum, accel0, factor),
         [pltpu.VMEM(whole, F32)],
     )
 
     def add(x, y, out):
         out[...] = x[...] + y[...]
 
-    (part,) = run(add, "add", [half], (keep, shot_swap(give, 1)))
+    (part,) = run(add, [half], (keep, shot_swap(give, 1)))
     bit = 2
     while bit < shots:
-        (part,) = run(add, "add", [half], (part, shot_swap(part, bit)))
+        (part,) = run(add, [half], (part, shot_swap(part, bit)))
         bit *= 2
 
     def gather(mine_ref, other_ref, total, squares):
@@ -593,9 +736,7 @@
                 acc += jnp.sum((value * value).reshape(width // 8, 8, lanes), axis=0)
         squares[...] = acc
 
-    total, squares = run(
-        gather, "gather", [whole, (8, lanes)], (part, shot_swap(part, 1))
-    )
+    total, squares = run(gather, [whole, (8, lanes)], (part, shot_swap(part, 1)))
 
     def add4(w, x, y, z, out):
         out[...] = (w[...] + x[...]) + (y[...] + z[...])
@@ -604,7 +745,7 @@
     others = []
     while bit < slabs:
         if others:
-            (squares,) = run(add4 if len(others) == 3 else add, "add_squares", [(8, lanes)], (squares, *others))
+            (squares,) = run(add4 if len(others) == 3 else add, [(8, lanes)], (squares, *others))
         if 2 * bit < slabs:
             others = [slab_swap(squares, k * bit) for k in (1, 2, 3)]
             bit *= 4
@@ -629,12 +770,7 @@
                 new_model[at] = model[at] - update_rate * (field[at] * inverse)
             gradient[p] = field[p, pl.ds(first, share)] * inverse
 
-    return run(
-        update,
-        "update",
-        [whole, (depth, share, lanes)],
-        (total, slowness, squares, *others),
-    )
+    return run(update, [whole, (depth, share, lanes)], (total, model, squares, *others))
 
 
 def solution(mesh):
@@ -652,10 +788,10 @@
         P(("groups", "shot"), None, None),
     )
     out_specs = (P(("groups", "slab"), None, None), P(("groups", "slab"), "shot", None))
+
+    def body(*args):
+        return tuple(per_device(*args))
+
     return jax.shard_map(
-        lambda *args: tuple(per_device(*args)),
-        mesh=mesh,
-        in_specs=in_specs,
-        out_specs=out_specs,
-        check_vma=False,
-    )
+        body, mesh=mesh, in_specs=in_specs, out_specs=out_specs, check_vma=False
+    )

time: 71.2 us -> 60.9 us (0.86)
  local copies, waits for them, and re-layouts: 7.24 us -> 0.01 us
  waiting for transfers between devices: 29.8 us -> 26.4 us
  starting transfers between devices: 21.8 us -> 22.9 us
    unnamed x30 -> x8, local copies, waits for them, and re-layouts: 7.24 us -> 0.01 us
    ppermute x14, waiting for transfers between devices: 17.4 us -> 15.3 us  [the longest x7 15.3 us: exchange(): got_a = lax.ppermute(sends[0], 'slab', pairs_a)]
    ppermute x3, waiting for transfers between devices: 4.01 us -> 2.77 us  [slab_swap(): return lax.ppermute(value, 'slab', [(i, i ^ bit) for i in range(slabs)])]
    ppermute x14, starting transfers between devices: 15.5 us -> 16.7 us  [the longest x7 16.5 us: exchange(): got_a = lax.ppermute(sends[0], 'slab', pairs_a)]
    pallas_call x18 -> x15, Pallas kernels: 11.3 us -> 10.7 us  [run(): pl.pallas_call(kernel, out_shape=[jax.ShapeDtypeStruct(shape, F32) for sh...]
  transfers between devices with their start and end apart: 21 -> 21, of which waited for: 12 -> 12; matrix products, arithmetic and copies ran while one was open for 0% -> 0% of each run, Pallas kernels for 11% -> 12%
where the time goes in v2:
time: 60.9 us; the launch traced here: 60.7 us
  waiting for transfers between devices  26.4 us (43%)
  starting transfers between devices  22.9 us (38%)
  Pallas kernels  10.7 us (18%)
  between operations  0.75 us (1%)
    ppermute x7, starting transfers between devices, exchange(): got_a = lax.ppermute(sends[0], 'slab', pairs_a)  16.5 us
    ppermute x7, waiting for transfers between devices, exchange(): got_a = lax.ppermute(sends[0], 'slab', pairs_a)  15.3 us
    pallas_call x15, Pallas kernels, run(): pl.pallas_call(kernel, out_shape=[jax.ShapeDtypeStruct(shape, F32) for sh...  10.7 us
    ppermute x4, waiting for transfers between devices, shot_swap(): return lax.ppermute(value, 'shot', [(i, i ^ bit) for i in range(shots)])  8.31 us
    ppermute x3, starting transfers between devices, slab_swap(): return lax.ppermute(value, 'slab', [(i, i ^ bit) for i in range(slabs)])  4.45 us
    ppermute x3, waiting for transfers between devices, slab_swap(): return lax.ppermute(value, 'slab', [(i, i ^ bit) for i in range(slabs)])  2.77 us
    ppermute x4, starting transfers between devices, shot_swap(): return lax.ppermute(value, 'shot', [(i, i ^ bit) for i in range(shots)])  1.77 us
  transfers between devices with their start and end apart: 21, of which 12 were waited for; matrix products, arithmetic and copies ran while one was open for 0% of the time, Pallas kernels for 12%

profile of v2, /device:TPU:0, one launch (start us, length us, event | category | flops | bytes accessed | tf_op | source)
XLA Modules:
  0.0 60.7 jit_solution(16087755479683069143)
XLA Ops:
  0.6 1.2 %shard_map.122 = (f32[3,192,128]{2,1,0:T(8,128)S(1)}, f32[3,192,128]{2,1,0:T(8,128)S(1)}) custom-call(f32[4,192,128]{2,1,0:T(8,128)} %bitcast.11, f32[4,192,128]{2,1,0:T(8,128)} %refs_4_.1), custom_call_target="tpu_custom_call" | custom-call | flops 200000 | bytes 200000 | tf_op jit(solution)/shard_map/pallas_call | solution.py:37
  1.8 3.1 %collective-permute-start = (f32[3,192,128]{2,1,0:T(8,128)S(1)}, f32[3,192,128]{2,1,0:T(8,128)S(1)}, u32[]{:S(2)}, u32[]{:S(2)}) collective-permute-start(f32[3,192,128]{2,1,0:T(8,128)S(1)} %get-tuple-element.70), channel_id=1, source_target_pairs={{0,1},{1,0},{2,3},{3,2},{4,5},{5,4},{6,7},{7,6},{8,9},{9,8},{10,11... | collective-permute-start | bytes 884744 | tf_op jit(solution)/shard_map/ppermute | solution.py:189
  4.9 0.0 collective-permute-start.1
  4.9 0.0 copy-start.2
  4.9 0.0 copy-start.3
  4.9 2.5 %shard_map.123 = (f32[4,192,128]{2,1,0:T(8,128)S(1)}, f32[4,192,128]{2,1,0:T(8,128)S(1)}, f32[4,192,128]{2,1,0:T(8,128)S(1)}, f32[4,192,128]{2,1,0:T(8,128)S(1)}...) custom-call(f32[4,192,128]{2,1,0:T(8,128)} %bitcast.12, ...), custom_call_target="tpu_custom_call" | custom-call | flops 200000 | bytes 200000 | tf_op jit(solution)/shard_map/pallas_call | solution.py:37
  7.4 0.0 copy-done.2
  7.4 0.0 copy-done.3
  7.5 1.6 %shard_map.124 = (f32[4,192,128]{2,1,0:T(8,128)S(1)}, f32[2,192,128]{2,1,0:T(8,128)S(1)}, f32[2,192,128]{2,1,0:T(8,128)S(1)}, f32[4,192,128]{2,1,0:T(8,128)S(1)}...) custom-call(s32[1,256]{1,0:T(1,128)S(1)} %bitcast.10, f32[4,256]{1,0:T(4,128)S(1)} %bitcast.9), custom_call_target="tpu_custom_call" | custom-call | flops 2000000 | bytes 2000000 | tf_op jit(solution)/shard_map/pallas_call | solution.py:37
  9.1 2.9 %collective-permute-done.a = f32[3,192,128]{2,1,0:T(8,128)S(1)} collective-permute-done((f32[3,192,128]{2,1,0:T(8,128)S(1)}, f32[3,192,128]{2,1,0:T(8,128)S(1)}, u32[]{:S(2)}, u32[]{:S(2)}) %collective-permute-start) | collective-permute-done | bytes 294944 | tf_op jit(solution)/shard_map/ppermute | solution.py:189
  11.9 0.0 collective-permute-done.1.b
  11.9 0.7 %shard_map.125 = (f32[2,192,128]{2,1,0:T(8,128)S(1)}, f32[4,192,128]{2,1,0:T(8,128)S(1)}, f32[4,192,128]{2,1,0:T(8,128)S(1)}, f32[4,192,128]{2,1,0:T(8,128)S(1)}...) custom-call(f32[3,192,128]{2,1,0:T(8,128)S(1)} %collective-permute-d, ...), custom_call_target="tpu_custom_call" | custom-call | flops 200000 | bytes 200000 | tf_op jit(solution)/shard_map/pallas_call | solution.py:37
  12.6 0.1 collective-permute-start.4
  12.7 2.9 %collective-permute-start.5 = (f32[2,192,128]{2,1,0:T(8,128)S(1)}, f32[2,192,128]{2,1,0:T(8,128)S(1)}, u32[]{:S(2)}, u32[]{:S(2)}) collective-permute-start(f32[2,192,128]{2,1,0:T(8,128)S(1)} %get-tuple-element.87), channel_id=1, source_target_pairs={{0,1},{1,0},{2,3},{3,2},{4,5},{5,4},{6,7},{7,6},{8,9},{9,8},{10,11... | collective-permute-start | bytes 589832 | tf_op jit(solution)/shard_map/ppermute | solution.py:189
  15.7 0.2 collective-permute-start.6
  15.8 1.9 %collective-permute-start.2 = (f32[2,192,128]{2,1,0:T(8,128)S(1)}, f32[2,192,128]{2,1,0:T(8,128)S(1)}, u32[]{:S(2)}, u32[]{:S(2)}) collective-permute-start(f32[2,192,128]{2,1,0:T(8,128)S(1)} %get-tuple-element.80), channel_id=1, source_target_pairs={{0,1},{1,0},{2,3},{3,2},{4,5},{5,4},{6,7},{7,6},{8,9},{9,8},{10,11... | collective-permute-start | bytes 589832 | tf_op jit(solution)/shard_map/ppermute | solution.py:189
  17.7 0.0 collective-permute-start.3
  17.7 0.0 collective-permute-done.4.other
  17.7 0.1 shard_map.126
  17.8 3.6 %collective-permute-done.5.a = f32[2,192,128]{2,1,0:T(8,128)S(1)} collective-permute-done((f32[2,192,128]{2,1,0:T(8,128)S(1)}, f32[2,192,128]{2,1,0:T(8,128)S(1)}, u32[]{:S(2)}, u32[]{:S(2)}) %collective-permute-start.5) | collective-permute-done | bytes 196640 | tf_op jit(solution)/shard_map/ppermute | solution.py:189
  21.4 0.0 collective-permute-done.6.b
  21.4 0.0 copy-start
  21.4 0.7 %shard_map.127 = (f32[4,192,128]{2,1,0:T(8,128)S(1)}, f32[4,192,128]{2,1,0:T(8,128)S(1)}, f32[4,192,128]{2,1,0:T(8,128)S(1)}, f32[4,192,128]{2,1,0:T(8,128)S(1)}...) custom-call(f32[2,192,128]{2,1,0:T(8,128)S(1)} %collective-permute-done.5.a, ...), custom_call_target="tpu_custom_call" | custom-call | flops 200000 | bytes 200000 | tf_op jit(solution)/shard_map/pallas_call | solution.py:37
  22.1 2.2 %collective-permute-start.9 = (f32[2,192,128]{2,1,0:T(8,128)S(1)}, f32[2,192,128]{2,1,0:T(8,128)S(1)}, u32[]{:S(2)}, u32[]{:S(2)}) collective-permute-start(f32[2,192,128]{2,1,0:T(8,128)S(1)} %get-tuple-element.107), channel_id=1, source_target_pairs={{0,1},{1,0},{2,3},{3,2},{4,5},{5,4},{6,7},{7,6},{8,9},{9,8},{10,11... | collective-permute-start | bytes 589832 | tf_op jit(solution)/shard_map/ppermute | solution.py:189
  24.2 0.0 collective-permute-start.10
  24.2 1.4 %collective-permute-done.2.a = f32[2,192,128]{2,1,0:T(8,128)S(1)} collective-permute-done((f32[2,192,128]{2,1,0:T(8,128)S(1)}, f32[2,192,128]{2,1,0:T(8,128)S(1)}, u32[]{:S(2)}, u32[]{:S(2)}) %collective-permute-start.2) | collective-permute-done | bytes 196640 | tf_op jit(solution)/shard_map/ppermute | solution.py:189
  25.6 0.0 collective-permute-done.3.b
  25.6 0.0 copy-done
  25.6 0.0 copy-start.1
  25.6 0.7 %shard_map.128 = (f32[4,192,128]{2,1,0:T(8,128)S(1)}, f32[4,192,128]{2,1,0:T(8,128)S(1)}, f32[4,192,128]{2,1,0:T(8,128)S(1)}, f32[4,192,128]{2,1,0:T(8,128)S(1)}...) custom-call(f32[2,192,128]{2,1,0:T(8,128)S(1)} %collective-permute-done.2.a, ...), custom_call_target="tpu_custom_call" | custom-call | flops 200000 | bytes 200000 | tf_op jit(solution)/shard_map/pallas_call | solution.py:37
  26.4 2.1 %collective-permute-start.7 = (f32[2,192,128]{2,1,0:T(8,128)S(1)}, f32[2,192,128]{2,1,0:T(8,128)S(1)}, u32[]{:S(2)}, u32[]{:S(2)}) collective-permute-start(f32[2,192,128]{2,1,0:T(8,128)S(1)} %get-tuple-element.102), channel_id=1, source_target_pairs={{0,1},{1,0},{2,3},{3,2},{4,5},{5,4},{6,7},{7,6},{8,9},{9,8},{10,11... | collective-permute-start | bytes 589832 | tf_op jit(solution)/shard_map/ppermute | solution.py:189
  28.5 0.0 collective-permute-start.8
  28.5 1.4 %collective-permute-done.9.a = f32[2,192,128]{2,1,0:T(8,128)S(1)} collective-permute-done((f32[2,192,128]{2,1,0:T(8,128)S(1)}, f32[2,192,128]{2,1,0:T(8,128)S(1)}, u32[]{:S(2)}, u32[]{:S(2)}) %collective-permute-start.9) | collective-permute-done | bytes 196640 | tf_op jit(solution)/shard_map/ppermute | solution.py:189
  30.0 0.0 collective-permute-done.10.b
  30.0 0.0 copy-done.1
  30.0 0.7 %shard_map.129 = (f32[4,192,128]{2,1,0:T(8,128)S(1)}, f32[4,192,128]{2,1,0:T(8,128)S(1)}, f32[4,192,128]{2,1,0:T(8,128)S(1)}, f32[4,192,128]{2,1,0:T(8,128)S(1)}...) custom-call(f32[2,192,128]{2,1,0:T(8,128)S(1)} %collective-permute-done.9.a, ...), custom_call_target="tpu_custom_call" | custom-call | flops 200000 | bytes 200000 | tf_op jit(solution)/shard_map/pallas_call | solution.py:37
  30.7 2.2 %collective-permute-start.13 = (f32[2,192,128]{2,1,0:T(8,128)S(1)}, f32[2,192,128]{2,1,0:T(8,128)S(1)}, u32[]{:S(2)}, u32[]{:S(2)}) collective-permute-start(f32[2,192,128]{2,1,0:T(8,128)S(1)} %get-tuple-element.123), channel_id=1, source_target_pairs={{0,1},{1,0},{2,3},{3,2},{4,5},{5,4},{6,7},{7,6},{8,9},{9,8},{10,11... | collective-permute-start | bytes 589832 | tf_op jit(solution)/shard_map/ppermute | solution.py:189
  32.8 0.0 collective-permute-start.14
  32.8 1.5 %collective-permute-done.7.a = f32[2,192,128]{2,1,0:T(8,128)S(1)} collective-permute-done((f32[2,192,128]{2,1,0:T(8,128)S(1)}, f32[2,192,128]{2,1,0:T(8,128)S(1)}, u32[]{:S(2)}, u32[]{:S(2)}) %collective-permute-start.7) | collective-permute-done | bytes 196640 | tf_op jit(solution)/shard_map/ppermute | solution.py:189
  34.3 0.0 collective-permute-done.8.b
  34.3 0.7 %shard_map.130 = (f32[4,192,128]{2,1,0:T(8,128)S(1)}, f32[4,192,128]{2,1,0:T(8,128)S(1)}, f32[4,192,128]{2,1,0:T(8,128)S(1)}, f32[4,192,128]{2,1,0:T(8,128)S(1)}...) custom-call(f32[2,192,128]{2,1,0:T(8,128)S(1)} %collective-permute-done.7.a, ...), custom_call_target="tpu_custom_call" | custom-call | flops 200000 | bytes 200000 | tf_op jit(solution)/shard_map/pallas_call | solution.py:37
  35.0 2.2 %collective-permute-start.11 = (f32[2,192,128]{2,1,0:T(8,128)S(1)}, f32[2,192,128]{2,1,0:T(8,128)S(1)}, u32[]{:S(2)}, u32[]{:S(2)}) collective-permute-start(f32[2,192,128]{2,1,0:T(8,128)S(1)} %get-tuple-element.120), channel_id=1, source_target_pairs={{0,1},{1,0},{2,3},{3,2},{4,5},{5,4},{6,7},{7,6},{8,9},{9,8},{10,11... | collective-permute-start | bytes 589832 | tf_op jit(solution)/shard_map/ppermute | solution.py:189
  37.1 0.0 collective-permute-start.12
  37.1 1.5 %collective-permute-done.13.a = f32[2,192,128]{2,1,0:T(8,128)S(1)} collective-permute-done((f32[2,192,128]{2,1,0:T(8,128)S(1)}, f32[2,192,128]{2,1,0:T(8,128)S(1)}, u32[]{:S(2)}, u32[]{:S(2)}) %collective-permute-start.13) | collective-permute-done | bytes 196640 | tf_op jit(solution)/shard_map/ppermute | solution.py:189
  38.6 0.0 collective-permute-done.14.b
  38.6 0.5 shard_map.131.acc
  39.1 3.1 %collective-permute-done.11.a = f32[2,192,128]{2,1,0:T(8,128)S(1)} collective-permute-done((f32[2,192,128]{2,1,0:T(8,128)S(1)}, f32[2,192,128]{2,1,0:T(8,128)S(1)}, u32[]{:S(2)}, u32[]{:S(2)}) %collective-permute-start.11) | collective-permute-done | bytes 196640 | tf_op jit(solution)/shard_map/ppermute | solution.py:189
  42.2 0.0 collective-permute-done.12.b
  42.2 0.2 shard_map.132
  42.4 0.1 collective-permute-start.15
  42.5 1.4 %collective-permute-done.15.y = f32[2,192,128]{2,1,0:T(8,128)S(1)} collective-permute-done((f32[2,192,128]{2,1,0:T(8,128)S(1)}, f32[2,192,128]{2,1,0:T(8,128)S(1)}, u32[]{:S(2)}, u32[]{:S(2)}) %collective-permute-start.15) | collective-permute-done | bytes 196640 | tf_op jit(solution)/shard_map/ppermute | solution.py:194
  44.0 1.6 %collective-permute-start.16 = (f32[2,192,128]{2,1,0:T(8,128)S(1)}, f32[2,192,128]{2,1,0:T(8,128)S(1)}, u32[]{:S(2)}, u32[]{:S(2)}) collective-permute-start(f32[2,192,128]{2,1,0:T(8,128)S(1)} %shard_map.133.x), channel_id=1, source_target_pairs={{0,8},{4,12},{8,0},{12,4},{1,9},{5,13},{9,1},{13,5},{2,10},{6,14},... | collective-permute-start | bytes 589832 | tf_op jit(solution)/shard_map/ppermute | solution.py:194
  45.5 5.5 %collective-permute-done.16.y = f32[2,192,128]{2,1,0:T(8,128)S(1)} collective-permute-done((f32[2,192,128]{2,1,0:T(8,128)S(1)}, f32[2,192,128]{2,1,0:T(8,128)S(1)}, u32[]{:S(2)}, u32[]{:S(2)}) %collective-permute-start.16) | collective-permute-done | bytes 196640 | tf_op jit(solution)/shard_map/ppermute | solution.py:194
  51.0 0.1 collective-permute-start.17
  51.1 1.4 %collective-permute-done.17.other_ref = f32[2,192,128]{2,1,0:T(8,128)S(1)} collective-permute-done((f32[2,192,128]{2,1,0:T(8,128)S(1)}, f32[2,192,128]{2,1,0:T(8,128)S(1)}, u32[]{:S(2)}, u32[]{:S(2)}) %collective-permute-start.17) | collective-permute-done | bytes 196640 | tf_op jit(solution)/shard_map/ppermute | solution.py:194
  52.5 0.1 shard_map.135
  52.6 2.7 %collective-permute-start.20 = (f32[8,128]{1,0:T(8,128)S(1)}, f32[8,128]{1,0:T(8,128)S(1)}, u32[]{:S(2)}, u32[]{:S(2)}) collective-permute-start(f32[8,128]{1,0:T(8,128)S(1)} %get-tuple-element.137.refs_0_), channel_id=1, source_target_pairs={{0,3},{1,2},{2,1},{3,0},{4,7},{5,6},{6,5},{7,4},{8,11},{9,10},{10,... | collective-permute-start | bytes 12296 | tf_op jit(solution)/shard_map/ppermute | solution.py:197
  55.3 0.6 collective-permute-start.19
  55.8 1.2 %collective-permute-start.18 = (f32[8,128]{1,0:T(8,128)S(1)}, f32[8,128]{1,0:T(8,128)S(1)}, u32[]{:S(2)}, u32[]{:S(2)}) collective-permute-start(f32[8,128]{1,0:T(8,128)S(1)} %get-tuple-element.137.refs_0_), channel_id=1, source_target_pairs={{0,1},{1,0},{2,3},{3,2},{4,5},{5,4},{6,7},{7,6},{8,9},{9,8},{10,11... | collective-permute-start | bytes 12296 | tf_op jit(solution)/shard_map/ppermute | solution.py:197
  57.0 1.0 %collective-permute-done.20.refs_3_ = f32[8,128]{1,0:T(8,128)S(1)} collective-permute-done((f32[8,128]{1,0:T(8,128)S(1)}, f32[8,128]{1,0:T(8,128)S(1)}, u32[]{:S(2)}, u32[]{:S(2)}) %collective-permute-start.20) | collective-permute-done | bytes 4128 | tf_op jit(solution)/shard_map/ppermute | solution.py:197
  58.0 1.7 %collective-permute-done.19.refs_2_ = f32[8,128]{1,0:T(8,128)S(1)} collective-permute-done((f32[8,128]{1,0:T(8,128)S(1)}, f32[8,128]{1,0:T(8,128)S(1)}, u32[]{:S(2)}, u32[]{:S(2)}) %collective-permute-start.19) | collective-permute-done | bytes 4128 | tf_op jit(solution)/shard_map/ppermute | solution.py:197
  59.8 0.0 collective-permute-done.18.refs_1_
  59.8 1.0 %shard_map.136 = (f32[4,192,128]{2,1,0:T(8,128)}, f32[4,48,128]{2,1,0:T(8,128)}) custom-call(f32[4,192,128]{2,1,0:T(8,128)S(1)} %get-tuple-element.135.field, f32[4,192,128]{2,1,0:T(8,128)S(1)} %get-tuple-element.136.model, f32[8,128]{1,0:T(8,128)S(1)} %get-tuple-element.137.refs_0_, f32[8,128]{1,0:T(8,128)S(1)} %collective-permute-done.18.refs_1_, ...), custom_call_target="tpu_custom_call" | custom-call | flops 200000 | bytes 200000 | tf_op jit(solution)/shard_map/pallas_call | solution.py:37
  (2 shorter events, 0.0 us)
Async XLA Ops:
  1.8 10.1 %collective-permute-start = (f32[3,192,128]{2,1,0:T(8,128)S(1)}, f32[3,192,128]{2,1,0:T(8,128)S(1)}, u32[]{:S(2)}, u32[]{:S(2)}) collective-permute-start(f32[3,192,128]{2,1,0:T(8,128)S(1)} %get-tuple-element.70), channel_id=1, source_target_pairs={{0,1},{1,0},{2,3},{3,2},{4,5},{5,4},{6,7},{7,6},{8,9},{9,8},{10,11... | collective-permute-start | bytes 884744 | tf_op jit(solution)/shard_map/ppermute | solution.py:189
  4.9 7.0 %collective-permute-start.1 = (f32[3,192,128]{2,1,0:T(8,128)S(1)}, f32[3,192,128]{2,1,0:T(8,128)S(1)}, u32[]{:S(2)}, u32[]{:S(2)}) collective-permute-start(f32[3,192,128]{2,1,0:T(8,128)S(1)} %get-tuple-element.71), channel_id=1, source_target_pairs={{0,4},{1,2},{2,1},{3,7},{4,0},{5,6},{6,5},{7,3},{8,12},{9,10},{10,... | collective-permute-start | bytes 884744 | tf_op jit(solution)/shard_map/ppermute | solution.py:190
  4.9 2.5 %copy-start.2 = (f32[1,4,256]{2,1,0:T(4,128)S(1)}, f32[1,4,256]{2,1,0:T(4,128)}, u32[]{:S(2)}) copy-start(f32[1,4,256]{2,1,0:T(4,128)} %param.21) | copy-start | bytes 12292
  4.9 2.5 %copy-start.3 = (s32[256]{0:T(256)S(1)}, s32[256]{0:T(256)}, u32[]{:S(2)}) copy-start(s32[256]{0:T(256)} %param.20) | copy-start | bytes 3076
  12.6 5.0 %collective-permute-start.4 = (f32[2,192,128]{2,1,0:T(8,128)S(1)}, f32[2,192,128]{2,1,0:T(8,128)S(1)}, u32[]{:S(2)}, u32[]{:S(2)}) collective-permute-start(f32[2,192,128]{2,1,0:T(8,128)S(1)} %get-tuple-element.83.mine), channel_id=1, source_target_pairs={{0,4},{4,0},{8,12},{12,8},{1,5},{5,1},{9,13},{13,9},{2,6},{6,2},{1... | collective-permute-start | bytes 589832 | tf_op jit(solution)/shard_map/ppermute | solution.py:194
  12.7 8.7 %collective-permute-start.5 = (f32[2,192,128]{2,1,0:T(8,128)S(1)}, f32[2,192,128]{2,1,0:T(8,128)S(1)}, u32[]{:S(2)}, u32[]{:S(2)}) collective-permute-start(f32[2,192,128]{2,1,0:T(8,128)S(1)} %get-tuple-element.87), channel_id=1, source_target_pairs={{0,1},{1,0},{2,3},{3,2},{4,5},{5,4},{6,7},{7,6},{8,9},{9,8},{10,11... | collective-permute-start | bytes 589832 | tf_op jit(solution)/shard_map/ppermute | solution.py:189
  15.7 5.8 %collective-permute-start.6 = (f32[2,192,128]{2,1,0:T(8,128)S(1)}, f32[2,192,128]{2,1,0:T(8,128)S(1)}, u32[]{:S(2)}, u32[]{:S(2)}) collective-permute-start(f32[2,192,128]{2,1,0:T(8,128)S(1)} %get-tuple-element.88), channel_id=1, source_target_pairs={{0,4},{1,2},{2,1},{3,7},{4,0},{5,6},{6,5},{7,3},{8,12},{9,10},{10,... | collective-permute-start | bytes 589832 | tf_op jit(solution)/shard_map/ppermute | solution.py:190
  15.8 9.8 %collective-permute-start.2 = (f32[2,192,128]{2,1,0:T(8,128)S(1)}, f32[2,192,128]{2,1,0:T(8,128)S(1)}, u32[]{:S(2)}, u32[]{:S(2)}) collective-permute-start(f32[2,192,128]{2,1,0:T(8,128)S(1)} %get-tuple-element.80), channel_id=1, source_target_pairs={{0,1},{1,0},{2,3},{3,2},{4,5},{5,4},{6,7},{7,6},{8,9},{9,8},{10,11... | collective-permute-start | bytes 589832 | tf_op jit(solution)/shard_map/ppermute | solution.py:189
  17.7 7.9 %collective-permute-start.3 = (f32[2,192,128]{2,1,0:T(8,128)S(1)}, f32[2,192,128]{2,1,0:T(8,128)S(1)}, u32[]{:S(2)}, u32[]{:S(2)}) collective-permute-start(f32[2,192,128]{2,1,0:T(8,128)S(1)} %get-tuple-element.81), channel_id=1, source_target_pairs={{0,4},{1,2},{2,1},{3,7},{4,0},{5,6},{6,5},{7,3},{8,12},{9,10},{10,... | collective-permute-start | bytes 589832 | tf_op jit(solution)/shard_map/ppermute | solution.py:190
  21.4 4.2 %copy-start = (f32[1,4,192,128]{3,2,1,0:T(8,128)S(1)}, f32[1,4,192,128]{3,2,1,0:T(8,128)}, u32[]{:S(2)}) copy-start(f32[1,4,192,128]{3,2,1,0:T(8,128)} %param.15) | copy-start | bytes 1179652
  22.1 7.9 %collective-permute-start.9 = (f32[2,192,128]{2,1,0:T(8,128)S(1)}, f32[2,192,128]{2,1,0:T(8,128)S(1)}, u32[]{:S(2)}, u32[]{:S(2)}) collective-permute-start(f32[2,192,128]{2,1,0:T(8,128)S(1)} %get-tuple-element.107), channel_id=1, source_target_pairs={{0,1},{1,0},{2,3},{3,2},{4,5},{5,4},{6,7},{7,6},{8,9},{9,8},{10,11... | collective-permute-start | bytes 589832 | tf_op jit(solution)/shard_map/ppermute | solution.py:189
  24.2 5.8 %collective-permute-start.10 = (f32[2,192,128]{2,1,0:T(8,128)S(1)}, f32[2,192,128]{2,1,0:T(8,128)S(1)}, u32[]{:S(2)}, u32[]{:S(2)}) collective-permute-start(f32[2,192,128]{2,1,0:T(8,128)S(1)} %get-tuple-element.108), channel_id=1, source_target_pairs={{0,4},{1,2},{2,1},{3,7},{4,0},{5,6},{6,5},{7,3},{8,12},{9,10},{10,... | collective-permute-start | bytes 589832 | tf_op jit(solution)/shard_map/ppermute | solution.py:190
  25.6 4.4 %copy-start.1 = (f32[1,4,192,128]{3,2,1,0:T(8,128)S(1)}, f32[1,4,192,128]{3,2,1,0:T(8,128)}, u32[]{:S(2)}) copy-start(f32[1,4,192,128]{3,2,1,0:T(8,128)} %param.16) | copy-start | bytes 1179652
  26.4 7.9 %collective-permute-start.7 = (f32[2,192,128]{2,1,0:T(8,128)S(1)}, f32[2,192,128]{2,1,0:T(8,128)S(1)}, u32[]{:S(2)}, u32[]{:S(2)}) collective-permute-start(f32[2,192,128]{2,1,0:T(8,128)S(1)} %get-tuple-element.102), channel_id=1, source_target_pairs={{0,1},{1,0},{2,3},{3,2},{4,5},{5,4},{6,7},{7,6},{8,9},{9,8},{10,11... | collective-permute-start | bytes 589832 | tf_op jit(solution)/shard_map/ppermute | solution.py:189
  28.5 5.8 %collective-permute-start.8 = (f32[2,192,128]{2,1,0:T(8,128)S(1)}, f32[2,192,128]{2,1,0:T(8,128)S(1)}, u32[]{:S(2)}, u32[]{:S(2)}) collective-permute-start(f32[2,192,128]{2,1,0:T(8,128)S(1)} %get-tuple-element.103), channel_id=1, source_target_pairs={{0,4},{1,2},{2,1},{3,7},{4,0},{5,6},{6,5},{7,3},{8,12},{9,10},{10,... | collective-permute-start | bytes 589832 | tf_op jit(solution)/shard_map/ppermute | solution.py:190
  30.7 7.9 %collective-permute-start.13 = (f32[2,192,128]{2,1,0:T(8,128)S(1)}, f32[2,192,128]{2,1,0:T(8,128)S(1)}, u32[]{:S(2)}, u32[]{:S(2)}) collective-permute-start(f32[2,192,128]{2,1,0:T(8,128)S(1)} %get-tuple-element.123), channel_id=1, source_target_pairs={{0,1},{1,0},{2,3},{3,2},{4,5},{5,4},{6,7},{7,6},{8,9},{9,8},{10,11... | collective-permute-start | bytes 589832 | tf_op jit(solution)/shard_map/ppermute | solution.py:189
  32.8 5.8 %collective-permute-start.14 = (f32[2,192,128]{2,1,0:T(8,128)S(1)}, f32[2,192,128]{2,1,0:T(8,128)S(1)}, u32[]{:S(2)}, u32[]{:S(2)}) collective-permute-start(f32[2,192,128]{2,1,0:T(8,128)S(1)} %get-tuple-element.124), channel_id=1, source_target_pairs={{0,4},{1,2},{2,1},{3,7},{4,0},{5,6},{6,5},{7,3},{8,12},{9,10},{10,... | collective-permute-start | bytes 589832 | tf_op jit(solution)/shard_map/ppermute | solution.py:190
  35.0 7.3 %collective-permute-start.11 = (f32[2,192,128]{2,1,0:T(8,128)S(1)}, f32[2,192,128]{2,1,0:T(8,128)S(1)}, u32[]{:S(2)}, u32[]{:S(2)}) collective-permute-start(f32[2,192,128]{2,1,0:T(8,128)S(1)} %get-tuple-element.120), channel_id=1, source_target_pairs={{0,1},{1,0},{2,3},{3,2},{4,5},{5,4},{6,7},{7,6},{8,9},{9,8},{10,11... | collective-permute-start | bytes 589832 | tf_op jit(solution)/shard_map/ppermute | solution.py:189
  37.1 5.1 %collective-permute-start.12 = (f32[2,192,128]{2,1,0:T(8,128)S(1)}, f32[2,192,128]{2,1,0:T(8,128)S(1)}, u32[]{:S(2)}, u32[]{:S(2)}) collective-permute-start(f32[2,192,128]{2,1,0:T(8,128)S(1)} %get-tuple-element.121), channel_id=1, source_target_pairs={{0,4},{1,2},{2,1},{3,7},{4,0},{5,6},{6,5},{7,3},{8,12},{9,10},{10,... | collective-permute-start | bytes 589832 | tf_op jit(solution)/shard_map/ppermute | solution.py:190
  42.4 1.5 %collective-permute-start.15 = (f32[2,192,128]{2,1,0:T(8,128)S(1)}, f32[2,192,128]{2,1,0:T(8,128)S(1)}, u32[]{:S(2)}, u32[]{:S(2)}) collective-permute-start(f32[2,192,128]{2,1,0:T(8,128)S(1)} %get-tuple-element.134), channel_id=1, source_target_pairs={{0,4},{4,0},{8,12},{12,8},{1,5},{5,1},{9,13},{13,9},{2,6},{6,2},{1... | collective-permute-start | bytes 589832 | tf_op jit(solution)/shard_map/ppermute | solution.py:194
  44.0 7.0 %collective-permute-start.16 = (f32[2,192,128]{2,1,0:T(8,128)S(1)}, f32[2,192,128]{2,1,0:T(8,128)S(1)}, u32[]{:S(2)}, u32[]{:S(2)}) collective-permute-start(f32[2,192,128]{2,1,0:T(8,128)S(1)} %shard_map.133.x), channel_id=1, source_target_pairs={{0,8},{4,12},{8,0},{12,4},{1,9},{5,13},{9,1},{13,5},{2,10},{6,14},... | collective-permute-start | bytes 589832 | tf_op jit(solution)/shard_map/ppermute | solution.py:194
  51.0 1.5 %collective-permute-start.17 = (f32[2,192,128]{2,1,0:T(8,128)S(1)}, f32[2,192,128]{2,1,0:T(8,128)S(1)}, u32[]{:S(2)}, u32[]{:S(2)}) collective-permute-start(f32[2,192,128]{2,1,0:T(8,128)S(1)} %shard_map.134.mine_ref), channel_id=1, source_target_pairs={{0,4},{4,0},{8,12},{12,8},{1,5},{5,1},{9,13},{13,9},{2,6},{6,2},{1... | collective-permute-start | bytes 589832 | tf_op jit(solution)/shard_map/ppermute | solution.py:194
  52.6 5.5 %collective-permute-start.20 = (f32[8,128]{1,0:T(8,128)S(1)}, f32[8,128]{1,0:T(8,128)S(1)}, u32[]{:S(2)}, u32[]{:S(2)}) collective-permute-start(f32[8,128]{1,0:T(8,128)S(1)} %get-tuple-element.137.refs_0_), channel_id=1, source_target_pairs={{0,3},{1,2},{2,1},{3,0},{4,7},{5,6},{6,5},{7,4},{8,11},{9,10},{10,... | collective-permute-start | bytes 12296 | tf_op jit(solution)/shard_map/ppermute | solution.py:197
  55.3 4.5 %collective-permute-start.19 = (f32[8,128]{1,0:T(8,128)S(1)}, f32[8,128]{1,0:T(8,128)S(1)}, u32[]{:S(2)}, u32[]{:S(2)}) collective-permute-start(f32[8,128]{1,0:T(8,128)S(1)} %get-tuple-element.137.refs_0_), channel_id=1, source_target_pairs={{0,2},{1,3},{2,0},{3,1},{4,6},{5,7},{6,4},{7,5},{8,10},{9,11},{10,... | collective-permute-start | bytes 12296 | tf_op jit(solution)/shard_map/ppermute | solution.py:197
  55.8 3.9 %collective-permute-start.18 = (f32[8,128]{1,0:T(8,128)S(1)}, f32[8,128]{1,0:T(8,128)S(1)}, u32[]{:S(2)}, u32[]{:S(2)}) collective-permute-start(f32[8,128]{1,0:T(8,128)S(1)} %get-tuple-element.137.refs_0_), channel_id=1, source_target_pairs={{0,1},{1,0},{2,3},{3,2},{4,5},{5,4},{6,7},{7,6},{8,9},{9,8},{10,11... | collective-permute-start | bytes 12296 | tf_op jit(solution)/shard_map/ppermute | solution.py:197
